TPU v7x, 128 devices: a whole 4x4x4 slice. The times are simulated.
128 devices in a mesh: group: 32 (over z, y, x_hi), head: 4 (over x_lo, core).
Axes of the slice: x: 4 (x_hi: 2, x_lo: 2; x = x_hi * 2 + x_lo), y: 4, z: 4, core: 2. Of those that a mesh axis runs over, the one named last changes fastest.
Arguments:
- tokens: bfloat16 [4, 4096, 1536], P(None, 'group'), may hold values from -6 to 6
- parents: int32 [3, 4096], P(None, 'group'), may hold values from 0 to 7
- page_request: int32 [1536], P('group'), may hold values from 0 to 511, as said below
- page_fill: int32 [1536], P('group'), may hold values from 1 to 128, as said below
- keys_pool: bfloat16 [1536, 1536, 128], P('group', 'head'), may hold values from -600 to 600
- values_pool: bfloat16 [1536, 1536, 128], P('group', 'head'), may hold values from -6 to 6
- decay_pool: bfloat16 [1536, 24, 128], P('group', 'head'), may hold values from -494.52 to 0
- gain_attn: float32 [1536], replicated, may hold values from 0.1 to 1.9
- w_query: bfloat16 [1536, 1536], P('head'), may hold values from -0.15625 to 0.15625
- w_key: bfloat16 [1536, 1536], P('head'), may hold values from -0.15625 to 0.15625
- w_value: bfloat16 [1536, 1536], P('head'), may hold values from -0.15625 to 0.15625
- w_forget: bfloat16 [1536, 24], P(None, 'head'), may hold values from -0.15625 to 0.15625
- forget_bias: float32 [24], P('head'), may hold values from -2 to 6
- w_out: bfloat16 [1536, 1536], P('head'), may hold values from -0.15625 to 0.15625
- gain_ffn: float32 [1536], replicated, may hold values from 0.1 to 1.9
- w_gate: bfloat16 [1536, 4096], P(None, 'head'), may hold values from -0.15625 to 0.15625
- w_up: bfloat16 [1536, 4096], P(None, 'head'), may hold values from -0.15625 to 0.15625
- w_down: bfloat16 [4096, 1536], P('head'), may hold values from -0.09375 to 0.09375
Outputs:
- outputs: bfloat16 [4, 4096, 1536], P(None, 'group')
Inputs may be any that keep to these rules, and one draw needn't show every extreme that they name: `page_request`: request ids g * 16 to g * 16 + 15 are the requests owned by group g, and pages g * 48 to g * 48 + 47 are the page slots of group g. The first 32 slots of a group hold pages of its own requests; its other 16 slots hold pages of other groups' requests, at most 1 from the requests of one group. Every request has at least one page. `page_fill`: the valid positions of a page are its first ones.
All inputs are finite; a program needn't handle non-finite values.
Results may differ from a plain program's by a relative error of at most 0.0095.
Values may be sent and summed in bfloat16 or wider, within the bound.
A program may use at most 192 MiB of HBM per device.

v0:
```python
import jax
import jax.numpy as jnp
from jax import lax
from jax.sharding import PartitionSpec as P

BEAMS = 8
OWNED_SLOTS = 32
SPILL = 16


epsilon = 1e-05
masked_score = -1e30


def rms_scale(values, gain_vector):
    widened = values.astype(jnp.float32)
    return (
        widened
        * lax.rsqrt(jnp.mean(widened * widened, axis=-1, keepdims=True) + epsilon)
        * gain_vector
    )


def page_partials(page_keys, page_values, page_decay, fill_count, asked_rows, head_count):
    page_count, inner_width, length = page_keys.shape
    head_size = inner_width // head_count
    keys_split = page_keys.reshape(page_count, head_count, head_size, length)
    values_split = page_values.reshape(page_count, head_count, head_size, length)
    asked_split = asked_rows.reshape(asked_rows.shape[:3] + (head_count, head_size))
    scores = jnp.einsum(
        "pbshd,phdt->pbsht", asked_split, keys_split, preferred_element_type=jnp.float32
    ) * head_size ** (-0.5)
    scores = scores + page_decay.astype(jnp.float32)[:, None, None, :, :]
    valid_mask = jnp.arange(length)[None, :] < fill_count[:, None]
    scores = jnp.where(valid_mask[:, None, None, None, :], scores, masked_score)
    page_top = jnp.max(scores, axis=-1)
    weights = jnp.exp(scores - page_top[..., None])
    page_total = jnp.sum(weights, axis=-1)
    numerator = jnp.einsum(
        "pbsht,phdt->pbshd",
        weights.astype(jnp.bfloat16),
        values_split,
        preferred_element_type=jnp.float32,
    )
    return (page_top, page_total, numerator.reshape(numerator.shape[:3] + (inner_width,)))


def by_request(current_request, page_top, page_total, numerator, request_count, head_count):
    matches = current_request[None, :] == jnp.arange(request_count)[:, None]
    wide_match = matches[:, :, None, None, None]
    best_top = jnp.max(jnp.where(wide_match, page_top[None], masked_score), axis=1)
    factor = jnp.where(wide_match, jnp.exp(page_top[None] - best_top[:, None]), 0.0)
    summed = jnp.sum(factor * page_total[None], axis=1)
    numer_split = numerator.reshape(numerator.shape[:3] + (head_count, -1))
    combined = jnp.sum(factor[..., None] * numer_split[None], axis=1)
    return (best_top, summed, combined.reshape(combined.shape[:3] + (-1,)))


def shards(
    tokens,
    parents,
    page_request,
    page_fill,
    keys_pool,
    values_pool,
    decay_pool,
    gain_attn,
    w_query,
    w_key,
    w_value,
    w_forget,
    forget_bias,
    w_out,
    gain_ffn,
    w_gate,
    w_up,
    w_down,
):
    step_count, row_count, model_width = tokens.shape
    head_count = w_forget.shape[1]
    inner_width = w_query.shape[0]
    head_size = inner_width // head_count
    local_count = row_count // BEAMS
    groups = lax.axis_size("group")
    own_group = lax.axis_index("group")
    capacity = (SPILL + groups - 2) // (groups - 1)
    flat_tokens = tokens.reshape(step_count * row_count, model_width)
    normed = rms_scale(flat_tokens, gain_attn).astype(jnp.bfloat16)

    def project(weight):
        product = lax.dot_general(
            normed, weight, (((1,), (1,)), ((), ())), preferred_element_type=jnp.float32
        )
        return product.astype(jnp.bfloat16).reshape(step_count, row_count, -1)

    queries = project(w_query)
    key_new = project(w_key)
    value_new = project(w_value)
    forget = jax.nn.log_sigmoid(
        jnp.dot(normed, w_forget, preferred_element_type=jnp.float32) + forget_bias
    ).reshape(step_count, row_count, head_count)
    by_row = queries.transpose(1, 0, 2)
    by_request_rows = by_row.reshape(local_count, BEAMS, step_count, inner_width)
    own_request = page_request[:OWNED_SLOTS] - own_group * local_count
    own_parts = page_partials(
        keys_pool[:OWNED_SLOTS],
        values_pool[:OWNED_SLOTS],
        decay_pool[:OWNED_SLOTS],
        page_fill[:OWNED_SLOTS],
        by_request_rows[own_request],
        head_count,
    )
    hosted_request = page_request[OWNED_SLOTS:]
    hosted_owner = hosted_request // local_count
    hosted_local = hosted_request % local_count
    hosted_index = jnp.arange(hosted_request.shape[0])
    earlier = (hosted_owner[:, None] == hosted_owner[None, :]) & (
        hosted_index[None, :] < hosted_index[:, None]
    )
    hosted_rank = jnp.sum(earlier, axis=1)
    slot_match = (hosted_owner[None, None, :] == jnp.arange(groups)[:, None, None]) & (
        hosted_rank[None, None, :] == jnp.arange(capacity)[None, :, None]
    )
    slot_full = jnp.any(slot_match, axis=2)
    slot_source = jnp.sum(jnp.where(slot_match, hosted_index[None, None, :], 0), axis=2)
    slot_local = jnp.sum(jnp.where(slot_match, hosted_local[None, None, :], 0), axis=2)
    slot_count = groups * capacity
    base_rows = jnp.arange(row_count) // BEAMS * BEAMS
    hist_keys = jnp.zeros((0, row_count, inner_width), jnp.bfloat16)
    hist_values = jnp.zeros((0, row_count, inner_width), jnp.bfloat16)
    hist_totals = jnp.zeros((0, row_count, head_count), jnp.float32)
    running = jnp.zeros((row_count, head_count), jnp.float32)
    finished = []
    for step_index in range(step_count):
        query_block = by_row[:, step_index : step_index + 1]
        step_span = query_block.shape[1]
        gathered = lax.all_gather(query_block, "group", axis=0, tiled=True)
        asked_rows = gathered.reshape(groups * local_count, BEAMS, step_span, inner_width)[
            hosted_request
        ]
        page_top, page_total, numerator = page_partials(
            keys_pool[OWNED_SLOTS:],
            values_pool[OWNED_SLOTS:],
            decay_pool[OWNED_SLOTS:],
            page_fill[OWNED_SLOTS:],
            asked_rows,
            head_count,
        )
        full_slot = slot_full[:, :, None, None, None]
        own_now = tuple((member[:, :, step_index : step_index + 1] for member in own_parts))
        all_request = jnp.concatenate(
            [
                own_request,
                lax.all_to_all(
                    slot_local.astype(jnp.float32), "group", split_axis=0, concat_axis=0, tiled=True
                )
                .reshape(slot_count)
                .astype(jnp.int32),
            ],
            axis=0,
        )
        all_top = jnp.concatenate(
            [
                own_now[0],
                lax.all_to_all(
                    jnp.where(full_slot, page_top[slot_source], masked_score),
                    "group",
                    split_axis=0,
                    concat_axis=0,
                    tiled=True,
                ).reshape((slot_count,) + page_top.shape[1:]),
            ],
            axis=0,
        )
        all_total = jnp.concatenate(
            [
                own_now[1],
                lax.all_to_all(
                    jnp.where(full_slot, page_total[slot_source], 0.0),
                    "group",
                    split_axis=0,
                    concat_axis=0,
                    tiled=True,
                ).reshape((slot_count,) + page_total.shape[1:]),
            ],
            axis=0,
        )
        all_numer = jnp.concatenate(
            [
                own_now[2],
                lax.all_to_all(
                    jnp.where(full_slot, numerator[slot_source], 0.0),
                    "group",
                    split_axis=0,
                    concat_axis=0,
                    tiled=True,
                ).reshape((slot_count,) + numerator.shape[1:]),
            ],
            axis=0,
        )
        page_top, page_total, page_numer = by_request(
            all_request, all_top, all_total, all_numer, local_count, head_count
        )
        page_top = page_top.reshape(row_count, head_count)
        page_total = page_total.reshape(row_count, head_count)
        page_numer = page_numer.reshape(row_count, head_count, head_size)
        if step_index > 0:
            source = base_rows + parents[step_index - 1]
            hist_keys = hist_keys[:, source]
            hist_values = hist_values[:, source]
            hist_totals = hist_totals[:, source]
            running = running[source]
        running = running + forget[step_index]
        hist_keys = jnp.concatenate([hist_keys, key_new[step_index][None]], axis=0)
        hist_values = jnp.concatenate([hist_values, value_new[step_index][None]], axis=0)
        hist_totals = jnp.concatenate([hist_totals, running[None]], axis=0)
        asked_now = queries[step_index].reshape(row_count, head_count, head_size)
        keys_now = hist_keys.reshape(step_index + 1, row_count, head_count, head_size)
        values_now = hist_values.reshape(step_index + 1, row_count, head_count, head_size)
        scores = jnp.einsum(
            "rhd,urhd->rhu", asked_now, keys_now, preferred_element_type=jnp.float32
        ) * head_size ** (-0.5) - hist_totals.transpose(1, 2, 0)
        history_top = jnp.max(scores, axis=-1)
        weights = jnp.exp(scores - history_top[..., None])
        history_total = jnp.sum(weights, axis=-1)
        history_numer = jnp.einsum(
            "rhu,urhd->rhd",
            weights.astype(jnp.bfloat16),
            values_now,
            preferred_element_type=jnp.float32,
        )
        best_top = jnp.maximum(page_top, history_top)
        page_scale = jnp.exp(page_top - best_top)
        history_scale = jnp.exp(history_top - best_top)
        total_sum = page_total * page_scale + history_total * history_scale
        numer_sum = page_numer * page_scale[..., None] + history_numer * history_scale[..., None]
        attended = (
            (numer_sum / total_sum[..., None]).astype(jnp.bfloat16).reshape(row_count, inner_width)
        )
        mixed_sum = lax.psum(jnp.dot(attended, w_out, preferred_element_type=jnp.float32), "head")
        residual = tokens[step_index].astype(jnp.float32) + mixed_sum
        normed_ffn = rms_scale(residual, gain_ffn).astype(jnp.bfloat16)
        gate_proj = jnp.dot(normed_ffn, w_gate, preferred_element_type=jnp.float32)
        up_proj = jnp.dot(normed_ffn, w_up, preferred_element_type=jnp.float32)
        hidden = (jax.nn.silu(gate_proj) * up_proj).astype(jnp.bfloat16)
        down_sum = lax.psum(jnp.dot(hidden, w_down, preferred_element_type=jnp.float32), "head")
        finished.append((residual + down_sum).astype(jnp.bfloat16))
    result = jnp.stack(finished, axis=0)
    return result


def solution(mesh):
    return jax.shard_map(
        shards,
        mesh=mesh,
        in_specs=(
            P(None, "group", None),
            P(None, "group"),
            P("group"),
            P("group"),
            P("group", "head", None),
            P("group", "head", None),
            P("group", "head", None),
            P(),
            P("head", None),
            P("head", None),
            P("head", None),
            P(None, "head"),
            P("head"),
            P("head", None),
            P(),
            P(None, "head"),
            P(None, "head"),
            P("head", None),
        ),
        out_specs=P(None, "group", None),
        check_vma=False,
    )
```

profile of v0, /device:TPU:1, one launch (start us, length us, event | category | flops | bytes accessed | tf_op | source)
XLA Modules:
  0.0 839.9 jit_solution(794505036848824269)
XLA Ops:
  19.0 11.5 %all-to-all-start = ((f32[32,1,1]{2,1,0:T(1,128)}), f32[32,1,1]{2,1,0:T(1,128)}, u32[]{:S(2)}, u32[]{:S(2)}) async-start(f32[32,1,1]{2,1,0:T(1,128)} %copy.715), calls=%async_computation | async-start | bytes 32768 | tf_op jit(solution)/shard_map/all_to_all | solution.py:154
  35.8 3.9 slice.193
  43.6 3.7 reshape.1148
  47.3 3.8 bitcast_reduce_fusion
  56.5 4.7 copy.728
  61.2 4.6 reshape.1155
  79.7 2.8 slice.202
  82.5 2.8 slice.198
  140.6 2.8 gather_fusion.23
  179.1 67.8 %all-gather.11.cloned.1.call-done = bf16[4096,1,384]{2,0,1:T(8,128)(2,1)} async-done(((bf16[128,1,384]{2,0,1:T(8,128)(2,1)}), bf16[4096,1,384]{2,0,1:T(8,128)(2,1)}) %all-gather.11.cloned.1.call-update) | async-done | bytes 3145744 | tf_op jit(solution)/shard_map/all_gather | solution.py:137
  254.5 3.3 fusion.162
  259.4 3.4 fusion.164
  270.3 3.3 convolution_bitcast_fusion.2
  277.1 46.8 %all-gather.5.cloned.1.call-done = bf16[4096,1,384]{2,0,1:T(8,128)(2,1)} async-done(((bf16[128,1,384]{2,0,1:T(8,128)(2,1)}), bf16[4096,1,384]{2,0,1:T(8,128)(2,1)}) %all-gather.5.cloned.1.call-update) | async-done | bytes 3145744 | tf_op jit(solution)/shard_map/all_gather | solution.py:137
  372.1 5.6 all-to-all-start.1
  377.7 3.2 convolution_bitcast_fusion.4
  400.3 9.2 %all-to-all-start.4 = ((f32[32,1,8,1,6]{2,3,4,1,0:T(1,128)}), f32[32,1,8,1,6]{2,3,4,1,0:T(1,128)S(1)}, u32[]{:S(2)}, u32[]{:S(2)}) async-start(f32[32,1,8,1,6]{2,3,4,1,0:T(1,128)} %copy.745), calls=%async_computation.4 | async-start | bytes 196608 | tf_op jit(solution)/shard_map/all_to_all | solution.py:165
  409.5 2.7 fusion.69
  418.4 8.4 all-to-all-start.7
  426.9 8.7 %all-to-all-done.7 = f32[32,1,8,1,6]{2,3,4,1,0:T(1,128)S(1)} async-done(((f32[32,1,8,1,6]{2,3,4,1,0:T(1,128)}), f32[32,1,8,1,6]{2,3,4,1,0:T(1,128)S(1)}, u32[]{:S(2)}, u32[]{:S(2)}) %all-to-all-start.7) | async-done | bytes 6176 | tf_op jit(solution)/shard_map/all_to_all | solution.py:165
  435.6 4.3 all-to-all-start.10
  441.5 6.9 all-to-all-done.10
  448.4 3.8 all-to-all-start.3
  453.8 7.3 all-to-all-done.3
  461.1 3.8 all-to-all-start.12
  465.9 8.0 all-to-all-done.12
  473.9 4.5 all-to-all-start.6
  481.4 5.9 all-to-all-done.6
  487.3 4.5 all-to-all-start.9
  503.8 9.2 %all-to-all-start.2 = ((f32[32,1,8,1,384]{4,2,3,1,0:T(8,128)}), f32[32,1,8,1,384]{4,2,3,1,0:T(8,128)S(1)}, u32[]{:S(2)}, u32[]{:S(2)}) async-start(f32[32,1,8,1,384]{4,2,3,1,0:T(8,128)} %get-tuple-element.103), calls=%async_computation.2 | async-start | bytes 786432 | tf_op jit(solution)/shard_map/all_to_all | solution.py:191
  530.5 7.8 exponential_select_fusion.1
  539.5 9.3 %all-to-all-start.5 = ((f32[32,1,8,1,384]{4,2,3,1,0:T(8,128)}), f32[32,1,8,1,384]{4,2,3,1,0:T(8,128)}, u32[]{:S(2)}, u32[]{:S(2)}) async-start(f32[32,1,8,1,384]{4,2,3,1,0:T(8,128)} %get-tuple-element.101), calls=%async_computation.5 | async-start | bytes 786432 | tf_op jit(solution)/shard_map/all_to_all | solution.py:191
  552.9 7.7 multiply_reduce_fusion.3
  561.9 9.2 %all-to-all-start.11 = ((f32[32,1,8,1,384]{4,2,3,1,0:T(8,128)}), f32[32,1,8,1,384]{4,2,3,1,0:T(8,128)S(1)}, u32[]{:S(2)}, u32[]{:S(2)}) async-start(f32[32,1,8,1,384]{4,2,3,1,0:T(8,128)} %get-tuple-element.102), calls=%async_computation.11 | async-start | bytes 786432 | tf_op jit(solution)/shard_map/all_to_all | solution.py:191
  577.7 7.7 multiply_reduce_fusion.2
  590.9 9.3 %all-to-all-start.8 = ((f32[32,1,8,1,384]{4,2,3,1,0:T(8,128)}), f32[32,1,8,1,384]{4,2,3,1,0:T(8,128)}, u32[]{:S(2)}, u32[]{:S(2)}) async-start(f32[32,1,8,1,384]{4,2,3,1,0:T(8,128)} %get-tuple-element.100), calls=%async_computation.8 | async-start | bytes 786432 | tf_op jit(solution)/shard_map/all_to_all | solution.py:191
  604.5 7.7 multiply_reduce_fusion
  620.3 7.7 multiply_reduce_fusion.1
  631.2 88.7 %all-reduce.7.cloned.1.call-done = (f32[128,1536]{1,0:T(8,128)}, f32[128,1536]{1,0:T(8,128)}, f32[128,1536]{1,0:T(8,128)}, f32[128,1536]{1,0:T(8,128)}) async-done(((f32[128,1536]{1,0:T(8,128)}, f32[128,1536]{1,0:T(8,128)}, f32[128,1536]{1,0:T(8,128)}, f32[128,1536]{1,0:T(8,128)}), (f32[128,1536]{1,0:T(8,128)}, f32[128,1536]{1,0:T(8,128)}, f32[128,1536]{1,0:T(8,128)}, ...) | async-done | bytes 3145744 | tf_op jit(solution)/shard_map/psum | solution.py:240
  719.9 3.0 multiply_reduce_fusion.10
  728.4 4.1 fusion.33
  732.5 4.1 fusion.34
  736.5 3.4 fusion.169
  740.0 4.1 fusion.35
  744.1 3.3 fusion.167
  747.3 4.0 fusion.36
  751.3 76.1 %all-reduce.5.cloned.1.call-done = (f32[128,1536]{1,0:T(8,128)}, f32[128,1536]{1,0:T(8,128)}, f32[128,1536]{1,0:T(8,128)}, f32[128,1536]{1,0:T(8,128)}) async-done(((f32[128,1536]{1,0:T(8,128)}, f32[128,1536]{1,0:T(8,128)}, f32[128,1536]{1,0:T(8,128)}, f32[128,1536]{1,0:T(8,128)}), (f32[128,1536]{1,0:T(8,128)}, f32[128,1536]{1,0:T(8,128)}, f32[128,1536]{1,0:T(8,128)}, ...) | async-done | bytes 3145744 | tf_op jit(solution)/shard_map/psum | solution.py:246
  827.4 4.1 fusion.58
  (463 shorter events, 302.7 us)
Async XLA Ops:
  6.5 721.9 %copy-start = (bf16[1024,1536]{1,0:T(8,128)(2,1)S(1)}, bf16[1024,1536]{1,0:T(8,128)(2,1)}, u32[]{:S(2)}) copy-start(bf16[1024,1536]{1,0:T(8,128)(2,1)} %param.35) | copy-start | bytes 9437188
  6.5 165.9 %all-gather.9.cloned.1.call-start = ((), (), s32[]{:S(2)}) async-start(), calls=%async_computation.15 | async-start | bytes 3244032 | tf_op jit(solution)/shard_map/all_gather | solution.py:137
  15.1 160.7 %all-gather.7.cloned.1.call-start = ((), (), s32[]{:S(2)}) async-start(), calls=%async_computation.14 | async-start | bytes 3244032 | tf_op jit(solution)/shard_map/all_gather | solution.py:137
  15.8 231.1 %all-gather.11.cloned.1.call-start = ((), (), s32[]{:S(2)}) async-start(), calls=%async_computation.16 | async-start | bytes 3244032 | tf_op jit(solution)/shard_map/all_gather | solution.py:137
  17.6 17.3 %copy-start.87 = (pred[16]{0:T(512)(128)(4,1)}, pred[16]{0:T(512)(128)(4,1)S(1)}, u32[]{:S(2)}) copy-start(pred[16]{0:T(512)(128)(4,1)S(1)} %broadcast_compare_fusion) | copy-start | bytes 52
  19.0 150.7 %all-to-all-start = ((f32[32,1,1]{2,1,0:T(1,128)}), f32[32,1,1]{2,1,0:T(1,128)}, u32[]{:S(2)}, u32[]{:S(2)}) async-start(f32[32,1,1]{2,1,0:T(1,128)} %copy.715), calls=%async_computation | async-start | bytes 32768 | tf_op jit(solution)/shard_map/all_to_all | solution.py:154
  30.4 293.4 %all-gather.5.cloned.1.call-start = ((), (), s32[]{:S(2)}) async-start(), calls=%async_computation.13 | async-start | bytes 3244032 | tf_op jit(solution)/shard_map/all_gather | solution.py:137
  87.7 21.9 %copy-start.39 = (f32[32,8,1,6]{1,2,3,0:T(1,128)S(1)}, f32[32,8,1,6]{1,2,3,0:T(1,128)}, u32[]{:S(2)}) copy-start(f32[32,8,1,6]{1,2,3,0:T(1,128)} %get-tuple-element.76) | copy-start | bytes 18436
  105.5 19.6 %copy-start.69 = (f32[128,6]{0,1:T(8,128)S(1)}, f32[128,6]{0,1:T(8,128)}, u32[]{:S(2)}) copy-start(f32[128,6]{0,1:T(8,128)} %copy.815) | copy-start | bytes 9220
  106.5 20.0 %copy-start.53 = (f32[128,6]{0,1:T(8,128)S(1)}, f32[128,6]{0,1:T(8,128)}, u32[]{:S(2)}) copy-start(f32[128,6]{0,1:T(8,128)} %slice_add_fusion.1) | copy-start | bytes 9220
  140.6 14.2 %copy-start.33 = (bf16[2,128,384]{1,2,0:T(8,128)(2,1)S(1)}, bf16[2,128,384]{1,2,0:T(8,128)(2,1)}, u32[]{:S(2)}) copy-start(bf16[2,128,384]{1,2,0:T(8,128)(2,1)} %copy.782) | copy-start | bytes 589828
  148.1 18.0 %copy-start.79 = (s32[16]{0:T(128)S(1)}, s32[16]{0:T(128)}, u32[]{:S(2)}) copy-start(s32[16]{0:T(128)} %copy-done.78) | copy-start | bytes 196
  166.1 226.7 %copy-start.56 = (s32[1024]{0:T(1024)}, s32[1024]{0:T(1024)S(1)}, u32[]{:S(2)}) copy-start(s32[1024]{0:T(1024)S(1)} %pad_clamp_fusion.3) | copy-start | bytes 12292
  264.4 10.9 %copy-start.30 = (f32[16,8,6]{1,2,0:T(8,128)S(1)}, f32[16,8,6]{1,2,0:T(8,128)}, u32[]{:S(2)}) copy-start(f32[16,8,6]{1,2,0:T(8,128)} %get-tuple-element.119) | copy-start | bytes 9220
  327.2 41.9 %copy-start.81 = (pred[32]{0:T(512)(128)(4,1)S(1)}, pred[32]{0:T(512)(128)(4,1)}, u32[]{:S(2)}) copy-start(pred[32]{0:T(512)(128)(4,1)} %fusion.115) | copy-start | bytes 100
  372.1 28.2 %all-to-all-start.1 = ((f32[32,1,8,1,6]{2,3,4,1,0:T(1,128)}), f32[32,1,8,1,6]{2,3,4,1,0:T(1,128)}, u32[]{:S(2)}, u32[]{:S(2)}) async-start(f32[32,1,8,1,6]{2,3,4,1,0:T(1,128)} %copy.724), calls=%async_computation.1 | async-start | bytes 196608 | tf_op jit(solution)/shard_map/all_to_all | solution.py:165
  388.3 21.1 %copy-start.82 = (pred[32]{0:T(512)(128)(4,1)S(1)}, pred[32]{0:T(512)(128)(4,1)}, u32[]{:S(2)}) copy-start(pred[32]{0:T(512)(128)(4,1)} %fusion.115) | copy-start | bytes 100
  394.1 19.5 %copy-start.49 = (f32[32,1,8,1,6]{0,2,4,3,1:T(8,128)S(1)}, f32[32,1,8,1,6]{0,2,4,3,1:T(8,128)}, u32[]{:S(2)}) copy-start(f32[32,1,8,1,6]{0,2,4,3,1:T(8,128)} %get-tuple-element.110) | copy-start | bytes 18436
  394.1 20.3 %copy-start.48 = (f32[32,1,8,1,6]{0,2,4,3,1:T(8,128)S(1)}, f32[32,1,8,1,6]{0,2,4,3,1:T(8,128)}, u32[]{:S(2)}) copy-start(f32[32,1,8,1,6]{0,2,4,3,1:T(8,128)} %get-tuple-element.107) | copy-start | bytes 18436
  394.1 21.0 %copy-start.47 = (f32[32,1,8,1,6]{0,2,4,3,1:T(8,128)S(1)}, f32[32,1,8,1,6]{0,2,4,3,1:T(8,128)}, u32[]{:S(2)}) copy-start(f32[32,1,8,1,6]{0,2,4,3,1:T(8,128)} %get-tuple-element.109) | copy-start | bytes 18436
  394.1 21.7 %copy-start.46 = (f32[32,1,8,1,6]{0,2,4,3,1:T(8,128)S(1)}, f32[32,1,8,1,6]{0,2,4,3,1:T(8,128)}, u32[]{:S(2)}) copy-start(f32[32,1,8,1,6]{0,2,4,3,1:T(8,128)} %get-tuple-element.104) | copy-start | bytes 18436
  396.0 30.8 %copy-start.44 = (f32[32,8,1,6]{0,1,3,2:T(8,128)S(1)}, f32[32,8,1,6]{0,1,3,2:T(8,128)}, u32[]{:S(2)}) copy-start(f32[32,8,1,6]{0,1,3,2:T(8,128)} %copy.726) | copy-start | bytes 18436
  396.0 30.8 %copy-start.45 = (f32[32,8,1,6]{0,1,3,2:T(8,128)S(1)}, f32[32,8,1,6]{0,1,3,2:T(8,128)}, u32[]{:S(2)}) copy-start(f32[32,8,1,6]{0,1,3,2:T(8,128)} %copy.747) | copy-start | bytes 18436
  397.2 55.7 %copy-start.42 = (f32[32,8,1,6]{0,1,3,2:T(8,128)S(1)}, f32[32,8,1,6]{0,1,3,2:T(8,128)}, u32[]{:S(2)}) copy-start(f32[32,8,1,6]{0,1,3,2:T(8,128)} %copy.773) | copy-start | bytes 18436
  397.2 55.7 %copy-start.43 = (f32[32,8,1,6]{0,1,3,2:T(8,128)S(1)}, f32[32,8,1,6]{0,1,3,2:T(8,128)}, u32[]{:S(2)}) copy-start(f32[32,8,1,6]{0,1,3,2:T(8,128)} %copy.805) | copy-start | bytes 18436
  398.8 13.4 %copy-start.51 = (f32[32,1,8,1,6]{0,2,4,3,1:T(8,128)S(1)}, f32[32,1,8,1,6]{0,2,4,3,1:T(8,128)}, u32[]{:S(2)}) copy-start(f32[32,1,8,1,6]{0,2,4,3,1:T(8,128)} %get-tuple-element.105) | copy-start | bytes 18436
  398.8 14.1 %copy-start.50 = (f32[32,1,8,1,6]{0,2,4,3,1:T(8,128)S(1)}, f32[32,1,8,1,6]{0,2,4,3,1:T(8,128)}, u32[]{:S(2)}) copy-start(f32[32,1,8,1,6]{0,2,4,3,1:T(8,128)} %get-tuple-element.108) | copy-start | bytes 18436
  400.3 18.1 %all-to-all-start.4 = ((f32[32,1,8,1,6]{2,3,4,1,0:T(1,128)}), f32[32,1,8,1,6]{2,3,4,1,0:T(1,128)S(1)}, u32[]{:S(2)}, u32[]{:S(2)}) async-start(f32[32,1,8,1,6]{2,3,4,1,0:T(1,128)} %copy.745), calls=%async_computation.4 | async-start | bytes 196608 | tf_op jit(solution)/shard_map/all_to_all | solution.py:165
  418.4 17.3 %all-to-all-start.7 = ((f32[32,1,8,1,6]{2,3,4,1,0:T(1,128)}), f32[32,1,8,1,6]{2,3,4,1,0:T(1,128)S(1)}, u32[]{:S(2)}, u32[]{:S(2)}) async-start(f32[32,1,8,1,6]{2,3,4,1,0:T(1,128)} %copy.771), calls=%async_computation.7 | async-start | bytes 196608 | tf_op jit(solution)/shard_map/all_to_all | solution.py:165
  426.9 76.8 %copy-start.34 = (f32[64,8,6]{0,1,2:T(8,128)}, f32[64,8,6]{0,1,2:T(8,128)S(1)}, u32[]{:S(2)}) copy-start(f32[64,8,6]{0,1,2:T(8,128)S(1)} %get-tuple-element.124) | copy-start | bytes 36868
  435.6 12.7 %all-to-all-start.10 = ((f32[32,1,8,1,6]{2,3,4,1,0:T(1,128)}), f32[32,1,8,1,6]{2,3,4,1,0:T(1,128)S(1)}, u32[]{:S(2)}, u32[]{:S(2)}) async-start(f32[32,1,8,1,6]{2,3,4,1,0:T(1,128)} %copy.803), calls=%async_computation.10 | async-start | bytes 196608 | tf_op jit(solution)/shard_map/all_to_all | solution.py:165
  440.8 62.9 %copy-start.27 = (f32[16,8,6]{1,2,0:T(8,128)}, f32[16,8,6]{1,2,0:T(8,128)S(1)}, u32[]{:S(2)}) copy-start(f32[16,8,6]{1,2,0:T(8,128)S(1)} %select_reduce_fusion.3) | copy-start | bytes 9220
  448.4 12.7 %all-to-all-start.3 = ((f32[32,1,8,1,6]{2,3,4,1,0:T(1,128)}), f32[32,1,8,1,6]{2,3,4,1,0:T(1,128)S(1)}, u32[]{:S(2)}, u32[]{:S(2)}) async-start(f32[32,1,8,1,6]{2,3,4,1,0:T(1,128)} %copy.737), calls=%async_computation.3 | async-start | bytes 196608 | tf_op jit(solution)/shard_map/all_to_all | solution.py:178
  453.8 50.0 %copy-start.35 = (f32[64,8,6]{0,1,2:T(8,128)}, f32[64,8,6]{0,1,2:T(8,128)S(1)}, u32[]{:S(2)}) copy-start(f32[64,8,6]{0,1,2:T(8,128)S(1)} %get-tuple-element.125) | copy-start | bytes 36868
  453.8 50.0 %copy-start.36 = (f32[64,8,6]{0,1,2:T(8,128)}, f32[64,8,6]{0,1,2:T(8,128)S(1)}, u32[]{:S(2)}) copy-start(f32[64,8,6]{0,1,2:T(8,128)S(1)} %get-tuple-element.126) | copy-start | bytes 36868
  461.1 12.8 %all-to-all-start.12 = ((f32[32,1,8,1,6]{2,3,4,1,0:T(1,128)}), f32[32,1,8,1,6]{2,3,4,1,0:T(1,128)S(1)}, u32[]{:S(2)}, u32[]{:S(2)}) async-start(f32[32,1,8,1,6]{2,3,4,1,0:T(1,128)} %copy.826), calls=%async_computation.12 | async-start | bytes 196608 | tf_op jit(solution)/shard_map/all_to_all | solution.py:178
  473.9 13.4 %all-to-all-start.6 = ((f32[32,1,8,1,6]{2,3,4,1,0:T(1,128)}), f32[32,1,8,1,6]{2,3,4,1,0:T(1,128)}, u32[]{:S(2)}, u32[]{:S(2)}) async-start(f32[32,1,8,1,6]{2,3,4,1,0:T(1,128)} %copy.763), calls=%async_computation.6 | async-start | bytes 196608 | tf_op jit(solution)/shard_map/all_to_all | solution.py:178
  480.4 23.4 %copy-start.24 = (f32[16,8,6]{1,2,0:T(8,128)}, f32[16,8,6]{1,2,0:T(8,128)S(1)}, u32[]{:S(2)}) copy-start(f32[16,8,6]{1,2,0:T(8,128)S(1)} %get-tuple-element.10) | copy-start | bytes 9220
  480.4 23.4 %copy-start.25 = (f32[16,8,6]{1,2,0:T(8,128)}, f32[16,8,6]{1,2,0:T(8,128)S(1)}, u32[]{:S(2)}) copy-start(f32[16,8,6]{1,2,0:T(8,128)S(1)} %get-tuple-element.11) | copy-start | bytes 9220
  480.4 23.4 %copy-start.26 = (f32[16,8,6]{1,2,0:T(8,128)}, f32[16,8,6]{1,2,0:T(8,128)S(1)}, u32[]{:S(2)}) copy-start(f32[16,8,6]{1,2,0:T(8,128)S(1)} %get-tuple-element.12) | copy-start | bytes 9220
  487.3 16.4 %all-to-all-start.9 = ((f32[32,1,8,1,6]{2,3,4,1,0:T(1,128)}), f32[32,1,8,1,6]{2,3,4,1,0:T(1,128)}, u32[]{:S(2)}, u32[]{:S(2)}) async-start(f32[32,1,8,1,6]{2,3,4,1,0:T(1,128)} %copy.794), calls=%async_computation.9 | async-start | bytes 196608 | tf_op jit(solution)/shard_map/all_to_all | solution.py:178
  503.8 35.7 %all-to-all-start.2 = ((f32[32,1,8,1,384]{4,2,3,1,0:T(8,128)}), f32[32,1,8,1,384]{4,2,3,1,0:T(8,128)S(1)}, u32[]{:S(2)}, u32[]{:S(2)}) async-start(f32[32,1,8,1,384]{4,2,3,1,0:T(8,128)} %get-tuple-element.103), calls=%async_computation.2 | async-start | bytes 786432 | tf_op jit(solution)/shard_map/all_to_all | solution.py:191
  539.5 22.4 %all-to-all-start.5 = ((f32[32,1,8,1,384]{4,2,3,1,0:T(8,128)}), f32[32,1,8,1,384]{4,2,3,1,0:T(8,128)}, u32[]{:S(2)}, u32[]{:S(2)}) async-start(f32[32,1,8,1,384]{4,2,3,1,0:T(8,128)} %get-tuple-element.101), calls=%async_computation.5 | async-start | bytes 786432 | tf_op jit(solution)/shard_map/all_to_all | solution.py:191
  561.9 28.9 %all-to-all-start.11 = ((f32[32,1,8,1,384]{4,2,3,1,0:T(8,128)}), f32[32,1,8,1,384]{4,2,3,1,0:T(8,128)S(1)}, u32[]{:S(2)}, u32[]{:S(2)}) async-start(f32[32,1,8,1,384]{4,2,3,1,0:T(8,128)} %get-tuple-element.102), calls=%async_computation.11 | async-start | bytes 786432 | tf_op jit(solution)/shard_map/all_to_all | solution.py:191
  590.9 24.4 %all-to-all-start.8 = ((f32[32,1,8,1,384]{4,2,3,1,0:T(8,128)}), f32[32,1,8,1,384]{4,2,3,1,0:T(8,128)}, u32[]{:S(2)}, u32[]{:S(2)}) async-start(f32[32,1,8,1,384]{4,2,3,1,0:T(8,128)} %get-tuple-element.100), calls=%async_computation.8 | async-start | bytes 786432 | tf_op jit(solution)/shard_map/all_to_all | solution.py:191
  600.2 119.6 %all-reduce.7.cloned.1.call-start = ((), (), s32[]{:S(2)}) async-start(), calls=%async_computation.18 | async-start | bytes 6291456 | tf_op jit(solution)/shard_map/psum | solution.py:240
  631.1 91.7 %copy-start.76 = (f32[1536]{0:T(1024)S(1)}, f32[1536]{0:T(1024)}, u32[]{:S(2)}) copy-start(f32[1536]{0:T(1024)} %param.32) | copy-start | bytes 18436
  631.2 196.3 %all-reduce.5.cloned.1.call-start = ((), (), s32[]{:S(2)}) async-start(), calls=%async_computation.17 | async-start | bytes 6291456 | tf_op jit(solution)/shard_map/psum | solution.py:246
  (63 other events, 326.7 us)
Sparse Core Ops, SparseCore 0:
  15.2 77.4 all-gather.8
  95.7 74.0 all-gather.6
  172.8 74.0 all-gather.10
  249.7 74.0 all-gather.4
  631.3 88.5 all-reduce.6
  751.5 75.9 all-reduce.4
where the time goes:
time: 854 us; the launch traced here: 840 us
  waiting for transfers between devices  319 us (37%)
  local copies, waits for them, and re-layouts  223 us (26%)
  other arithmetic  123 us (14%)
  starting transfers between devices  93.1 us (11%)
  matrix products  66.5 us (8%)
  between operations  14.9 us (2%)
    all_gather x4, waiting for transfers between devices, shards(): gathered = lax.all_gather(query_block, 'group', axis=0, tiled=True)  115 us
    psum x1, waiting for transfers between devices, shards(): lax.psum(jnp.dot(attended, w_out, preferred_element_type=jnp.float32), 'h...  88.7 us
    psum x1, waiting for transfers between devices, shards(): lax.psum(jnp.dot(hidden, w_down, preferred_element_type=jnp.float32), 'he...  76.1 us
    all_to_all x4, starting transfers between devices, shards(): lax.all_to_all(jnp.where(full_slot, numerator[slot_source], 0.0), 'group'...  37 us
    reduce_sum x4, other arithmetic, by_request(): combined = jnp.sum(factor[..., None] * numer_split[None], axis=1)  30.9 us
    all_to_all x4, starting transfers between devices, shards(): lax.all_to_all(jnp.where(full_slot, page_top[slot_source], masked_score),...  27.4 us
    all_to_all x4, waiting for transfers between devices, shards(): lax.all_to_all(jnp.where(full_slot, page_total[slot_source], 0.0), 'group...  21.2 us
  transfers between devices with their start and end apart: 19, of which 11 were waited for; matrix products, arithmetic and copies ran while one was open for 36% of the time, Pallas kernels for 0%

commit v1 on v0

v1 whole, which is shorter than its diff:
```python
import functools

import jax
import jax.numpy as jnp
from jax import lax
from jax.experimental import pallas as pl
from jax.experimental.pallas import tpu as pltpu
from jax.sharding import PartitionSpec as P

BEAMS = 8
OWNED_SLOTS = 32
SPILL = 16
STAT = 128
EPS = 1e-05
MASKED = -1e30
F32 = jnp.float32
BF16 = jnp.bfloat16
MESH = pl.DeviceIdType.MESH


def rms(x, gain):
    return x * lax.rsqrt(jnp.mean(x * x, axis=-1, keepdims=True) + EPS) * gain


def dot(a, b):
    return jnp.dot(a, b, preferred_element_type=F32)


def dot_nt(a, b):
    return lax.dot_general(a, b, (((1,), (1,)), ((), ())), preferred_element_type=F32)


def exact_dot(a, b):
    return jnp.dot(a, b, preferred_element_type=F32, precision=lax.Precision.HIGHEST)


def iota(shape, dim):
    return lax.broadcasted_iota(jnp.int32, shape, dim)


def greet(peers):
    barrier = pltpu.get_barrier_semaphore()
    count = 0
    for peer in peers:
        pl.semaphore_signal(barrier, inc=1, device_id=peer, device_id_type=MESH)
        count += 1
    pl.semaphore_wait(barrier, count)


def greet_group(groups, me):
    barrier = pltpu.get_barrier_semaphore()

    def signal(d, c):
        peer = lax.rem(me + d, groups)
        pl.semaphore_signal(barrier, inc=1, device_id={"group": peer}, device_id_type=MESH)
        return c

    lax.fori_loop(1, groups, signal, 0)
    pl.semaphore_wait(barrier, groups - 1)


def front_kernel(
    groups,
    steps,
    local,
    tokens,
    table,
    gain,
    wq,
    wk,
    wv,
    wf,
    bias,
    q_req,
    q_step,
    k_out,
    v_out,
    f_out,
    q_in,
    loc_out,
    normed,
    table_in,
    send,
    wbuf,
    wsem,
    tsend,
    trecv,
    qsend,
    qrecv,
):
    me = lax.axis_index("group")
    rows = local * BEAMS
    width = q_step.shape[-1]
    loads = [pltpu.make_async_copy(w, wbuf.at[i], wsem.at[i]) for i, w in enumerate((wq, wk, wv))]
    for load in loads:
        load.start()
    greet_group(groups, me)

    def table_copy(d, there):
        return pltpu.make_async_remote_copy(
            src_ref=table,
            dst_ref=table_in.at[there],
            send_sem=tsend.at[d],
            recv_sem=trecv.at[there],
            device_id={"group": lax.rem(me + d, groups)},
            device_id_type=MESH,
        )

    def send_table(d, c):
        table_copy(d, me).start()
        return c

    lax.fori_loop(1, groups, send_table, 0)
    table_in[pl.ds(me, 1)] = jnp.full((1,) + table_in.shape[1:], -1, jnp.int32)

    def norm_step(t, c):
        x = tokens[t].astype(F32)
        normed[t] = rms(x, gain[...]).astype(BF16)
        return c

    lax.fori_loop(0, steps, norm_step, 0)
    loads[0].wait()

    def query_step(t, c):
        q = dot_nt(normed[t], wbuf[0])
        q_step[t] = q.astype(BF16)
        return c

    lax.fori_loop(0, steps, query_step, 0)
    by_request = (
        q_step[...]
        .astype(F32)
        .reshape(steps, local, BEAMS, width)
        .transpose(1, 0, 2, 3)
        .reshape(local, steps * BEAMS, width)
    )
    q_req[...] = by_request.astype(BF16)

    def wait_table(d, c):
        table_copy(d, lax.rem(me + d, groups)).wait_recv()
        return c

    lax.fori_loop(1, groups, wait_table, 0)
    span = steps * BEAMS
    batch = 8
    flat = q_req[...].reshape(local * span, width)

    def select_batch(i, c):
        heard = table_in[pl.ds(i * batch, batch)]
        mine = heard // local == me
        where = jnp.max(jnp.where(mine, heard - me * local, -1), axis=-1, keepdims=True)
        loc_out[pl.ds(i * batch, batch)] = jnp.broadcast_to(where, (batch, 8, 128))
        tall = jnp.concatenate([where] * (span // 8), axis=1)
        shape = (batch, span, local * span)
        hit = iota(shape, 2) - iota(shape, 1) == tall * span
        pick = jnp.where(hit, 1.0, 0.0).astype(BF16).reshape(batch * span, local * span)
        send[pl.ds(i * batch, batch)] = dot(pick, flat).astype(BF16).reshape(batch, span, width)
        return c

    lax.fori_loop(0, groups // batch, select_batch, 0)

    def query_copy(d, there):
        peer = lax.rem(me + d, groups)
        return pltpu.make_async_remote_copy(
            src_ref=send.at[peer],
            dst_ref=q_in.at[there],
            send_sem=qsend.at[d],
            recv_sem=qrecv.at[there],
            device_id={"group": peer},
            device_id_type=MESH,
        )

    def send_query(d, c):
        query_copy(d, me).start()
        return c

    lax.fori_loop(1, groups, send_query, 0)
    q_in[pl.ds(me, 1)] = jnp.zeros((1,) + q_in.shape[1:], BF16)
    loads[1].wait()
    loads[2].wait()

    def rest_step(t, c):
        x = normed[t]
        k_out[t] = dot_nt(x, wbuf[1]).astype(BF16)
        v_out[t] = dot_nt(x, wbuf[2]).astype(BF16)
        gate = jax.nn.log_sigmoid(dot(x, wf[...]) + bias[...])
        heads = gate.shape[-1]
        spread = jnp.where(iota((heads, width), 1) // (width // heads) == iota((heads, width), 0), 1.0, 0.0)
        f_out[t] = exact_dot(gate, spread)
        return c

    lax.fori_loop(0, steps, rest_step, 0)

    def finish(d, c):
        table_copy(d, me).wait_send()
        query_copy(d, me).wait_send()
        query_copy(d, lax.rem(me + d, groups)).wait_recv()
        return c

    lax.fori_loop(1, groups, finish, 0)


def page_partial(q, keys, values, decay, fill, heads):
    span, width = q.shape
    low = iota((span, 128), 1) < 64
    bias = jnp.where(iota((heads, 128), 1) < fill, decay.astype(F32), MASKED)
    numer, top, total, tops, totals = [], [], [], [], []
    for j in range(width // 128):
        cut = slice(128 * j, 128 * (j + 1))
        part = q[:, cut].astype(F32) * 0.125
        wide = jnp.concatenate([jnp.where(low, part, 0.0), jnp.where(low, 0.0, part)], axis=0)
        scores = dot(wide.astype(BF16), keys[cut])
        shift = jnp.concatenate(
            [
                jnp.broadcast_to(bias[2 * j : 2 * j + 1], (span, 128)),
                jnp.broadcast_to(bias[2 * j + 1 : 2 * j + 2], (span, 128)),
            ],
            axis=0,
        )
        scores = scores + shift
        best = jnp.max(scores, axis=-1, keepdims=True)
        weight = jnp.exp(scores - best)
        whole = jnp.sum(weight, axis=-1, keepdims=True)
        out = dot_nt(weight.astype(BF16), values[cut])
        numer.append(jnp.where(low, out[:span], out[span:]))
        best = jnp.broadcast_to(best, (2 * span, 128))
        whole = jnp.broadcast_to(whole, (2 * span, 128))
        top.append(jnp.where(low, best[:span], best[span:]))
        total.append(jnp.where(low, whole[:span], whole[span:]))
        tops += [best[:span], best[span:]]
        totals += [whole[:span], whole[span:]]
    return numer, top, total, tops, totals


def pack_stats(tops, totals):
    span = tops[0].shape[0]
    lane = iota((span, STAT), 1)
    head, kind = lane % 8, lane // 8
    top = jnp.zeros((span, STAT), F32)
    total = jnp.zeros((span, STAT), F32)
    for h, (a, b) in enumerate(zip(tops, totals)):
        top = jnp.where(head == h, a, top)
        total = jnp.where(head == h, b, total)
    value = jnp.where(kind < 3, top, total)
    first = value.astype(BF16).astype(F32)
    rest = value - first
    second = rest.astype(BF16).astype(F32)
    third = rest - second
    pick = jnp.where(kind < 3, kind, kind - 3)
    out = jnp.where(pick == 0, first, jnp.where(pick == 1, second, third))
    return jnp.where(kind < 6, out, 0.0)


def attend_kernel(
    per_step, own_steps, local, heads, request, fill, q_req, q_in, keys, values, decay,
    numer_out, top_out, total_out, send_out,
):
    step = pl.program_id(0)
    width = q_req.shape[-1]
    span = q_req.shape[1]
    blocks = width // 128

    @pl.when(step == 0)
    def _():
        numer_out[...] = jnp.zeros_like(numer_out)
        top_out[...] = jnp.full_like(top_out, MASKED)
        total_out[...] = jnp.zeros_like(total_out)
        lane = iota((send_out.shape[0], span, STAT), 2)
        send_out[:, :, :width] = jnp.zeros((send_out.shape[0], span, width), BF16)
        send_out[:, :, width:] = jnp.where(lane < 8, MASKED, 0.0).astype(BF16)

    own_base = lax.axis_index("group") * local

    def own_page(i, c):
        page = step * per_step + i
        where = request[page] - own_base
        numer, top, total, _, _ = page_partial(
            q_req[where], keys.at[i], values.at[i], decay[i], fill[page], heads
        )
        for j in range(blocks):
            cut = pl.ds(128 * j, 128)
            old = top_out[where, :, cut]
            best = jnp.maximum(old, top[j])
            keep = jnp.exp(old - best)
            add = jnp.exp(top[j] - best)
            numer_out[where, :, cut] = numer_out[where, :, cut] * keep + numer[j] * add
            total_out[where, :, cut] = total_out[where, :, cut] * keep + total[j] * add
            top_out[where, :, cut] = best
        return c

    def hosted_page(i, c):
        page = step * per_step + i
        owner = request[page] // local
        numer, _, _, tops, totals = page_partial(
            q_in[owner], keys.at[i], values.at[i], decay[i], fill[page], heads
        )
        for j in range(blocks):
            send_out[owner, :, 128 * j : 128 * (j + 1)] = numer[j].astype(BF16)
        send_out[owner, :, width:] = pack_stats(tops, totals).astype(BF16)
        return c

    @pl.when(step < own_steps)
    def _():
        lax.fori_loop(0, per_step, own_page, 0)

    @pl.when(step >= own_steps)
    def _():
        lax.fori_loop(0, per_step, hosted_page, 0)


def history(q, k, v, f, parents, numer_out, top_out, total_out, heads):
    steps, rows, width = q.shape
    size = width // heads
    square = (width, width)
    same = jnp.where(iota(square, 0) // size == iota(square, 1) // size, 1.0, 0.0).astype(BF16)
    keys, vals, sums = [], [], []
    for t in range(steps):
        if t > 0:
            lane = iota((rows, rows), 1)
            source = lane - lane % BEAMS + parents[t - 1 : t]
            pick = jnp.where(iota((rows, rows), 0) == source, 1.0, 0.0).T
            pick16 = pick.astype(BF16)
            keys = [dot(pick16, a).astype(BF16) for a in keys]
            vals = [dot(pick16, a).astype(BF16) for a in vals]
            sums = [exact_dot(pick, a) for a in sums]
        keys.append(k[t])
        vals.append(v[t])
        sums.append(f[t] + sums[-1] if t > 0 else f[t])
        asked = q[t].astype(F32)
        scores = []
        for key, total in zip(keys, sums):
            product = asked * key.astype(F32)
            high = product.astype(BF16)
            low = (product - high.astype(F32)).astype(BF16)
            scores.append((dot(high, same) + dot(low, same)) * size ** (-0.5) - total)
        best = functools.reduce(jnp.maximum, scores)
        weights = [jnp.exp(s - best) for s in scores]
        top_out[t] = best
        total_out[t] = functools.reduce(jnp.add, weights)
        numer_out[t] = functools.reduce(
            jnp.add, [w.astype(BF16).astype(F32) * a.astype(F32) for w, a in zip(weights, vals)]
        )


def return_kernel(
    groups, heads, sent, q, k, v, f, parents, arrived, numer_out, top_out, total_out, ssem, rsem
):
    me = lax.axis_index("group")
    greet_group(groups, me)

    def copy(d, there):
        peer = lax.rem(me + d, groups)
        return pltpu.make_async_remote_copy(
            src_ref=sent.at[peer],
            dst_ref=arrived.at[there],
            send_sem=ssem.at[d],
            recv_sem=rsem.at[there],
            device_id={"group": peer},
            device_id_type=MESH,
        )

    def start(d, c):
        copy(d, me).start()
        return c

    lax.fori_loop(1, groups, start, 0)
    arrived[pl.ds(me, 1)] = jnp.zeros((1,) + arrived.shape[1:], BF16)
    history(q, k, v, f, parents, numer_out, top_out, total_out, heads)

    def finish(d, c):
        copy(d, me).wait_send()
        copy(d, lax.rem(me + d, groups)).wait_recv()
        return c

    lax.fori_loop(1, groups, finish, 0)


def combine_kernel(
    heads, where, arrived, numer_in, top_in, total_in, h_numer, h_top, h_total,
    out, numer, top, total, stats, final,
):
    groups, span, full = arrived.shape
    local, _, width = numer_in.shape
    steps = h_numer.shape[0]
    size = width // heads
    numer[...] = numer_in[...]
    top[...] = top_in[...]
    total[...] = total_in[...]
    shape = (STAT, 2 * width)
    lane, col = iota(shape, 0), iota(shape, 1)
    second = jnp.where(col >= width, 1, 0)
    spread = (lane // 8 // 3 == second) & (lane % 8 == (col - second * width) // size)
    spread = jnp.where(spread, 1.0, 0.0).astype(BF16)
    batch = 8

    def expand(i, c):
        block = arrived[pl.ds(i * batch, batch), :, width:].reshape(batch * span, STAT)
        stats[pl.ds(i * batch, batch)] = dot(block, spread).reshape(batch, span, 2 * width)
        return c

    lax.fori_loop(0, groups // batch, expand, 0)

    def absorb(g, c):
        r = where[g]

        @pl.when(r >= 0)
        def _():
            old = top[r]
            new = stats[g, :, :width]
            best = jnp.maximum(old, new)
            keep = jnp.exp(old - best)
            add = jnp.exp(new - best)
            numer[r] = numer[r] * keep + arrived[g, :, :width].astype(F32) * add
            total[r] = total[r] * keep + stats[g, :, width:] * add
            top[r] = best

        return c

    lax.fori_loop(0, groups, absorb, 0)

    def close(r, c):
        cut = pl.ds(pl.multiple_of(r * BEAMS, BEAMS), BEAMS)
        shape = (steps, BEAMS, width)
        p_top = top[r].reshape(shape)
        best = jnp.maximum(p_top, h_top[:, cut])
        p_scale = jnp.exp(p_top - best)
        h_scale = jnp.exp(h_top[:, cut] - best)
        whole = total[r].reshape(shape) * p_scale + h_total[:, cut] * h_scale
        mixed = numer[r].reshape(shape) * p_scale + h_numer[:, cut] * h_scale
        final[:, cut] = mixed / whole
        return c

    lax.fori_loop(0, local, close, 0)
    out[...] = final[...].astype(BF16)


def tail_kernel(
    att, tokens, gain, wo_h, wg_h, wu_h, wd_h, out,
    wo, wg, wu, wd, keep, resid, normed, acc,
    a_tx, a_rx, b_tx, b_rx, c_tx, c_rx, d_tx, d_rx,
    wsem, sems_s, sems_r,
):
    steps, rows, model = out.shape
    half = rows // 2
    me = lax.axis_index("head")
    core = lax.rem(me, 2)
    sibling = {"head": me + 1 - 2 * core}
    chip = me // 2
    across = {"head": core + 2 * (1 - chip)}
    mine = pl.ds(pl.multiple_of(core * half, half), half)
    theirs = pl.ds(pl.multiple_of((1 - core) * half, half), half)
    loads = [
        pltpu.make_async_copy(a, b, wsem.at[i])
        for i, (a, b) in enumerate(((wo_h, wo), (wg_h, wg), (wu_h, wu), (wd_h, wd)))
    ]
    for load in loads:
        load.start()
    greet((sibling, across))

    def remote(kind, t, src, dst, device):
        return pltpu.make_async_remote_copy(
            src_ref=src,
            dst_ref=dst,
            send_sem=sems_s.at[kind, t],
            recv_sem=sems_r.at[kind, t],
            device_id=device,
            device_id_type=MESH,
        )

    copy_a = lambda t: remote(0, t, a_tx.at[t], a_rx.at[t], sibling)
    copy_b = lambda t: remote(1, t, b_tx.at[t], b_rx.at[t], across)
    copy_n = lambda t: remote(2, t, normed.at[t, mine], normed.at[t, mine], sibling)
    copy_n_in = lambda t: remote(2, t, normed.at[t, theirs], normed.at[t, theirs], sibling)
    copy_c = lambda t: remote(3, t, c_tx.at[t], c_rx.at[t], sibling)
    copy_d = lambda t: remote(4, t, d_tx.at[t], d_rx.at[t], across)
    copy_o = lambda t: remote(5, t, out.at[t, mine], out.at[t, mine], sibling)
    copy_o_in = lambda t: remote(5, t, out.at[t, theirs], out.at[t, theirs], sibling)

    loads[0].wait()

    def project(t, c):
        acc[...] = dot(att[t], wo[...])
        keep[t] = acc[mine]
        a_tx[t] = acc[theirs].astype(BF16)
        copy_a(t).start()
        return c

    lax.fori_loop(0, steps, project, 0)

    def cross(t, c):
        copy_a(t).wait_recv()
        b_tx[t] = (keep[t] + a_rx[t].astype(F32)).astype(BF16)
        copy_b(t).start()
        return c

    lax.fori_loop(0, steps, cross, 0)
    for load in loads[1:]:
        load.wait()

    def down_cross(t):
        copy_c(t).wait_recv()
        d_tx[t] = (keep[t] + c_rx[t].astype(F32)).astype(BF16)
        copy_d(t).start()

    def feed(t, c):
        copy_b(t).wait_recv()
        res = tokens[t, mine].astype(F32) + (b_tx[t].astype(F32) + b_rx[t].astype(F32))
        resid[t] = res
        normed[t, mine] = rms(res, gain[...]).astype(BF16)
        copy_n(t).start()

        @pl.when(t > 0)
        def _():
            down_cross(t - 1)

        copy_n_in(t).wait_recv()
        x = normed[t]
        gate = dot(x, wg[...])
        up = dot(x, wu[...])
        hidden = (gate / (1.0 + jnp.exp(-gate)) * up).astype(BF16)
        acc[...] = dot(hidden, wd[...])
        keep[t] = acc[mine]
        c_tx[t] = acc[theirs].astype(BF16)
        copy_c(t).start()
        return c

    lax.fori_loop(0, steps, feed, 0)
    down_cross(steps - 1)

    def close(t, c):
        copy_d(t).wait_recv()
        total = resid[t] + (d_tx[t].astype(F32) + d_rx[t].astype(F32))
        out[t, mine] = total.astype(BF16)
        copy_o(t).start()
        return c

    lax.fori_loop(0, steps, close, 0)

    def finish(t, c):
        copy_o_in(t).wait_recv()
        copy_a(t).wait_send()
        copy_b(t).wait_send()
        copy_n(t).wait_send()
        copy_c(t).wait_send()
        copy_d(t).wait_send()
        copy_o(t).wait_send()
        return c

    lax.fori_loop(0, steps, finish, 0)


VM = pl.BlockSpec(memory_space=pltpu.VMEM)
SM = pl.BlockSpec(memory_space=pltpu.SMEM)
HB = pl.BlockSpec(memory_space=pl.ANY)
DMA = pltpu.SemaphoreType.DMA
LIMIT = 56 << 20


def params(**kw):
    return pltpu.CompilerParams(vmem_limit_bytes=LIMIT, **kw)


def shards(
    tokens, parents, page_request, page_fill, keys_pool, values_pool, decay_pool, gain_attn,
    w_query, w_key, w_value, w_forget, forget_bias, w_out, gain_ffn, w_gate, w_up, w_down,
):
    steps, rows, model = tokens.shape
    heads = w_forget.shape[1]
    width = w_query.shape[0]
    local = rows // BEAMS
    span = steps * BEAMS
    groups = lax.axis_size("group")
    pages = page_request.shape[0]
    ff = w_gate.shape[1]
    sds = jax.ShapeDtypeStruct

    hosted = jnp.full((8, 128), -1, jnp.int32).at[:, :SPILL].set(page_request[OWNED_SLOTS:][None])
    q_req, q_step, k_new, v_new, f_new, q_in, loc = pl.pallas_call(
        functools.partial(front_kernel, groups, steps, local),
        out_shape=(
            sds((local, span, width), BF16),
            sds((steps, rows, width), BF16),
            sds((steps, rows, width), BF16),
            sds((steps, rows, width), BF16),
            sds((steps, rows, width), F32),
            sds((groups, span, width), BF16),
            sds((groups, 8, 128), jnp.int32),
        ),
        in_specs=[VM, VM, VM, HB, HB, HB, VM, VM],
        out_specs=(VM,) * 7,
        scratch_shapes=[
            pltpu.VMEM((steps, rows, model), BF16),
            pltpu.VMEM((groups, 8, 128), jnp.int32),
            pltpu.VMEM((groups, span, width), BF16),
            pltpu.VMEM((3, width, model), BF16),
            DMA((3,)),
            DMA((groups,)),
            DMA((groups,)),
            DMA((groups,)),
            DMA((groups,)),
        ],
        compiler_params=params(collective_id=0, has_side_effects=True),
        name="front",
    )(tokens, hosted, gain_attn[None], w_query, w_key, w_value, w_forget, forget_bias[None])

    per_step = 8
    whole = lambda shape: pl.BlockSpec(shape, lambda i, *_: (0,) * len(shape))
    paged = lambda shape: pl.BlockSpec((per_step,) + shape, lambda i, *_: (i, 0, 0))
    state = (local, span, width)
    p_numer, p_top, p_total, sent = pl.pallas_call(
        functools.partial(attend_kernel, per_step, OWNED_SLOTS // per_step, local, heads),
        out_shape=(sds(state, F32),) * 3 + (sds((groups, span, width + STAT), BF16),),
        grid_spec=pltpu.PrefetchScalarGridSpec(
            num_scalar_prefetch=2,
            grid=(pages // per_step,),
            in_specs=[
                whole(state),
                whole((groups, span, width)),
                paged(keys_pool.shape[1:]),
                paged(values_pool.shape[1:]),
                paged(decay_pool.shape[1:]),
            ],
            out_specs=(whole(state),) * 3 + (whole((groups, span, width + STAT)),),
        ),
        compiler_params=params(),
        name="attend",
    )(page_request, page_fill, q_req, q_in, keys_pool, values_pool, decay_pool)

    arrived, h_numer, h_top, h_total = pl.pallas_call(
        functools.partial(return_kernel, groups, heads),
        out_shape=(sds((groups, span, width + STAT), BF16),) + (sds((steps, rows, width), F32),) * 3,
        in_specs=[VM] * 6,
        out_specs=(VM,) * 4,
        scratch_shapes=[DMA((groups,)), DMA((groups,))],
        compiler_params=params(collective_id=1, has_side_effects=True),
        name="bring",
    )(sent, q_step, k_new, v_new, f_new, parents)

    attended = pl.pallas_call(
        functools.partial(combine_kernel, heads),
        out_shape=sds((steps, rows, width), BF16),
        in_specs=[SM] + [VM] * 7,
        out_specs=VM,
        scratch_shapes=[pltpu.VMEM(state, F32)] * 3
        + [pltpu.VMEM((groups, span, 2 * width), F32), pltpu.VMEM((steps, rows, width), F32)],
        compiler_params=params(),
        name="combine",
    )(loc[:, 0, 0], arrived, p_numer, p_top, p_total, h_numer, h_top, h_total)

    half = (steps, rows // 2, model)
    return pl.pallas_call(
        tail_kernel,
        out_shape=sds((steps, rows, model), BF16),
        in_specs=[VM, VM, VM, HB, HB, HB, HB],
        out_specs=VM,
        scratch_shapes=[
            pltpu.VMEM((width, model), BF16),
            pltpu.VMEM((model, ff), BF16),
            pltpu.VMEM((model, ff), BF16),
            pltpu.VMEM((ff, model), BF16),
            pltpu.VMEM(half, F32),
            pltpu.VMEM(half, F32),
            pltpu.VMEM((steps, rows, model), BF16),
            pltpu.VMEM((rows, model), F32),
        ]
        + [pltpu.VMEM(half, BF16)] * 8
        + [DMA((4,)), DMA((6, steps)), DMA((6, steps))],
        compiler_params=params(collective_id=2, has_side_effects=True),
        name="tail",
    )(attended, tokens, gain_ffn[None], w_out, w_gate, w_up, w_down)


def solution(mesh):
    return jax.shard_map(
        shards,
        mesh=mesh,
        in_specs=(
            P(None, "group", None),
            P(None, "group"),
            P("group"),
            P("group"),
            P("group", "head", None),
            P("group", "head", None),
            P("group", "head", None),
            P(),
            P("head", None),
            P("head", None),
            P("head", None),
            P(None, "head"),
            P("head"),
            P("head", None),
            P(),
            P(None, "head"),
            P(None, "head"),
            P("head", None),
        ),
        out_specs=P(None, "group", None),
        check_vma=False,
    )
```

time: 854 us -> 148 us (0.17); the launches traced: 840 us -> 147 us
  waiting for transfers between devices: 319 us -> 0 us
  local copies, waits for them, and re-layouts: 223 us -> 9.68 us
  Pallas kernels: 0 us -> 136 us
  other arithmetic: 123 us -> 2.01 us
  starting transfers between devices: 93.1 us -> 0 us
  matrix products: 66.5 us -> 0 us
  between operations: 14.9 us -> 0.04 us
    psum x2 -> x0, waiting for transfers between devices: 165 us -> none  [the longest x1 88.7 us: shards(): lax.psum(jnp.dot(attended, w_out, preferred_element_type=jnp.float32), 'h...]
    pallas_call x0 -> x5, Pallas kernels: none -> 136 us  [the longest x1 43.1 us: shards(): pl.pallas_call(tail_kernel, out_shape=sds((steps, rows, model), BF16), in...]
    all_gather x4 -> x0, waiting for transfers between devices: 115 us -> none  [shards(): gathered = lax.all_gather(query_block, 'group', axis=0, tiled=True)]
    all_to_all x13 -> x0, starting transfers between devices: 92.7 us -> none  [the longest x4 37 us: shards(): lax.all_to_all(jnp.where(full_slot, numerator[slot_source], 0.0), 'group'...]
    gather x46 -> x0, local copies, waits for them, and re-layouts: 70.5 us -> none  [the longest x8 14.7 us: shards(): page_top[slot_source]]
    dot_general x26 -> x0, matrix products: 66.5 us -> none  [the longest x4 16.2 us: shards(): jnp.dot(hidden, w_down, preferred_element_type=jnp.float32)]
    reduce_sum x18 -> x0, other arithmetic: 54.2 us -> none  [the longest x4 30.9 us: by_request(): combined = jnp.sum(factor[..., None] * numer_split[None], axis=1)]
    all_to_all x13 -> x0, waiting for transfers between devices: 37.9 us -> none  [the longest x4 21.2 us: shards(): lax.all_to_all(jnp.where(full_slot, page_total[slot_source], 0.0), 'group...]
  transfers between devices with their start and end apart: 19 -> 0, of which waited for: 11 -> 0; matrix products, arithmetic and copies ran while one was open for 36% -> 0% of each run, Pallas kernels for 0% -> 0%
where the time goes in v1:
time: 148 us; the launch traced here: 147 us
  Pallas kernels  136 us (92%)
  local copies, waits for them, and re-layouts  9.68 us (7%)
  other arithmetic  2.01 us (1%)
    pallas_call x1, Pallas kernels, shards(): pl.pallas_call(tail_kernel, out_shape=sds((steps, rows, model), BF16), in...  43.1 us
    pallas_call x1, Pallas kernels, shards(): pl.pallas_call(functools.partial(attend_kernel, per_step, OWNED_SLOTS //...  32 us
    pallas_call x1, Pallas kernels, shards(): pl.pallas_call(functools.partial(front_kernel, groups, steps, local), out...  31.2 us
    pallas_call x1, Pallas kernels, shards(): pl.pallas_call(functools.partial(return_kernel, groups, heads), out_shape...  23.3 us
    pallas_call x1, Pallas kernels, shards(): pl.pallas_call(functools.partial(combine_kernel, heads), out_shape=sds((s...  6.08 us
    unnamed x7, local copies, waits for them, and re-layouts  5.02 us

profile of v1, /device:TPU:1, one launch (start us, length us, event | category | flops | bytes accessed | tf_op | source)
XLA Modules:
  0.0 147.4 jit_solution(11986333401613196812)
XLA Ops:
  0.0 0.6 compare_reduce_fusion
  0.6 1.4 broadcast_select_fusion
  2.0 0.6 scatter.8.table
  2.6 1.3 broadcast_in_dim.6.gain
  3.9 1.7 %copy.21.wf = bf16[1536,6]{1,0:T(8,128)(2,1)} copy(bf16[1536,6]{0,1:T(8,128)(2,1)} %param.31) | data formatting | bytes 36864 | tf_op args[11]
  5.6 0.0 copy-start
  5.6 31.2 %front.1 = (bf16[16,32,384]{2,1,0:T(8,128)(2,1)}, bf16[4,128,384]{2,1,0:T(8,128)(2,1)}, bf16[4,128,384]{2,1,0:T(8,128)(2,1)}, bf16[4,128,384]{2,1,0:T(8,128)(2,1...) custom-call(bf16[4,128,1536]{2,1,0:T(8,128)(2,1)} %tokens.3, ...), custom_call_target="tpu_custom_call" | custom-call | tf_op jit(solution)/shard_map/front/pallas_call | solution.py:578
  36.8 2.2 %slice_reduce_fusion.where = s32[32]{0:T(128)} fusion(s32[32,8,128]{2,1,0:T(8,128)} %get-tuple-element.32), kind=kLoop, calls=%fused_computation | loop fusion | bytes 256 | tf_op jit(solution)/shard_map/slice | solution.py:648
  39.0 0.0 copy-done
  39.0 0.7 copy.22.decay
  39.7 32.0 %attend.1 = (f32[16,32,384]{2,1,0:T(8,128)}, f32[16,32,384]{2,1,0:T(8,128)}, f32[16,32,384]{2,1,0:T(8,128)}, bf16[32,32,512]{2,1,0:T(8,128)(2,1)}) custom-call(s32[48]{0:T(128)} %request.1, s32[48]{0:T(128)} %fill.1, bf16[16,32,384]{2,1,0:T(8,128)(2,1)} %get-tuple-element.33.q_req, bf16[32,32,384]{2,1,0:T(8,128)(2,1)} %get-tuple-element.34.q_in, ...), custom_call_target="tpu_custom_call" | custom-call | tf_op jit(solution)/shard_map/attend/pallas_call | solution.py:610
  71.6 23.3 %bring.1 = (bf16[32,32,512]{2,1,0:T(8,128)(2,1)}, f32[4,128,384]{2,1,0:T(8,128)}, f32[4,128,384]{2,1,0:T(8,128)}, f32[4,128,384]{2,1,0:T(8,128)}) custom-call(bf16[32,32,512]{2,1,0:T(8,128)(2,1)} %get-tuple-element.35.sent, bf16[4,128,384]{2,1,0:T(8,128)(2,1)} %get-tuple-element.36.q, bf16[4,128,384]{2,1,0:T(8,128)(2,1)} %get-tuple-element.37.k, ...), custom_call_target="tpu_custom_call" | custom-call | tf_op jit(solution)/shard_map/bring/pallas_call | solution.py:629
  94.9 0.0 copy-start.1
  94.9 6.1 %combine.1.att = bf16[4,128,384]{2,1,0:T(8,128)(2,1)} custom-call(s32[32]{0:T(128)} %slice_reduce_fusion.where, bf16[32,32,512]{2,1,0:T(8,128)(2,1)} %get-tuple-element.40.arrived, f32[16,32,384]{2,1,0:T(8,128)} %get-tuple-element.41.numer_in, f32[16,32,384]{2,1,0:T(8,128)} %get-tuple-element.42.top_in, f32[16,32,384]{2,1,0:T(8,128)} %get-tuple-element.43.total_in, ...), custom_call_target="tpu_custom_call" | custom-call | tf_op jit(solution)/shard_map/combine/pallas_call | solution.py:639
  101.0 0.0 copy-done.1
  101.0 0.6 broadcast_in_dim.16.gain
  101.6 43.1 %tail.1 = bf16[4,128,1536]{2,1,0:T(8,128)(2,1)} custom-call(bf16[4,128,384]{2,1,0:T(8,128)(2,1)} %combine.1.att, bf16[4,128,1536]{2,1,0:T(8,128)(2,1)} %tokens.3, f32[1,1536]{1,0:T(1,128)} %broadcast_in_dim.16.gain, bf16[384,1536]{1,0:T(8,128)(2,1)} %wo_h.1, bf16[1536,1024]{1,0:T(8,128)(2,1)} %wg_h.1, bf16[1536,1024]{1,0:T(8,128)(2,1)} %wu_h.1, ...), custom_call_target="tpu_custom_call" | custom-call | tf_op jit(solution)/shard_map/tail/pallas_call | solution.py:651
  144.7 2.7 %copy.24 = bf16[4,128,1536]{2,1,0:T(8,128)(2,1)} copy(bf16[4,128,1536]{2,1,0:T(8,128)(2,1)} %tail.1) | data formatting | bytes 3145728
  (1 shorter events, 0.0 us)
Async XLA Ops:
  5.6 33.4 %copy-start = (bf16[48,6,128]{2,0,1:T(8,128)(2,1)S(1)}, bf16[48,6,128]{2,0,1:T(8,128)(2,1)}, u32[]{:S(2)}) copy-start(bf16[48,6,128]{2,0,1:T(8,128)(2,1)} %param.26) | copy-start | bytes 221188
  94.9 6.1 %copy-start.1 = (f32[1536]{0:T(1024)S(1)}, f32[1536]{0:T(1024)}, u32[]{:S(2)}) copy-start(f32[1536]{0:T(1024)} %param.34) | copy-start | bytes 18436

commit v2 on v1

v2 whole, which is shorter than its diff:
```python
import functools

import jax
import jax.numpy as jnp
from jax import lax
from jax.experimental import pallas as pl
from jax.experimental.pallas import tpu as pltpu
from jax.sharding import PartitionSpec as P

BEAMS = 8
OWNED_SLOTS = 32
SPILL = 16
STAT = 128
EPS = 1e-05
MASKED = -1e30
F32 = jnp.float32
BF16 = jnp.bfloat16
MESH = pl.DeviceIdType.MESH


def rms(x, gain):
    return x * lax.rsqrt(jnp.mean(x * x, axis=-1, keepdims=True) + EPS) * gain


def dot(a, b):
    return jnp.dot(a, b, preferred_element_type=F32)


def dot_nt(a, b):
    return lax.dot_general(a, b, (((1,), (1,)), ((), ())), preferred_element_type=F32)


def exact_dot(a, b):
    return jnp.dot(a, b, preferred_element_type=F32, precision=lax.Precision.HIGHEST)


def iota(shape, dim):
    return lax.broadcasted_iota(jnp.int32, shape, dim)


def greet(peers):
    barrier = pltpu.get_barrier_semaphore()
    count = 0
    for peer in peers:
        pl.semaphore_signal(barrier, inc=1, device_id=peer, device_id_type=MESH)
        count += 1
    pl.semaphore_wait(barrier, count)


def greet_group(groups, me):
    barrier = pltpu.get_barrier_semaphore()

    def signal(d, c):
        peer = lax.rem(me + d, groups)
        pl.semaphore_signal(barrier, inc=1, device_id={"group": peer}, device_id_type=MESH)
        return c

    lax.fori_loop(1, groups, signal, 0)
    pl.semaphore_wait(barrier, groups - 1)


def page_partial(q, masks, keys, values, bias):
    span, width = q.shape
    low = iota((span, 128), 1) < 64
    numer, top, total, tops, totals = [], [], [], [], []
    for j in range(width // 128):
        cut = slice(128 * j, 128 * (j + 1))
        wide = jnp.concatenate([q[:, cut]] * 2, axis=0) * masks
        shift = jnp.concatenate([jnp.broadcast_to(b, (span, 128)) for b in bias[2 * j : 2 * j + 2]], axis=0)
        scores = dot(wide, keys[cut]) + shift
        best = jnp.max(scores, axis=-1, keepdims=True)
        weight = jnp.exp(scores - best)
        whole = jnp.sum(weight, axis=-1, keepdims=True)
        out = dot(weight.astype(BF16), values[cut].astype(F32).T.astype(BF16))
        numer.append(jnp.where(low, out[:span], out[span:]))
        best = jnp.broadcast_to(best, (2 * span, 128))
        whole = jnp.broadcast_to(whole, (2 * span, 128))
        top.append(jnp.where(low, best[:span], best[span:]))
        total.append(jnp.where(low, whole[:span], whole[span:]))
        tops += [best[:span], best[span:]]
        totals += [whole[:span], whole[span:]]
    return numer, top, total, tops, totals


def pack_stats(tops, totals):
    span = tops[0].shape[0]
    lane = iota((span, STAT), 1)
    head, kind = lane % 8, lane // 8
    value = jnp.zeros((span, STAT), F32)
    for h, (a, b) in enumerate(zip(tops, totals)):
        value = jnp.where(head == h, jnp.where(kind < 3, a, b), value)
    first = value.astype(BF16).astype(F32)
    rest = value - first
    second = rest.astype(BF16).astype(F32)
    third = rest - second
    pick = jnp.where(kind < 3, kind, kind - 3)
    out = jnp.where(pick == 0, first, jnp.where(pick == 1, second, third))
    return jnp.where(kind < 6, out, 0.0)


def history(q, k, v, f, parents, numer_out, top_out, total_out, heads):
    steps, rows, width = q.shape
    size = width // heads
    square = (width, width)
    same = jnp.where(iota(square, 0) // size == iota(square, 1) // size, 1.0, 0.0).astype(BF16)
    keys, vals, sums = [], [], []
    for t in range(steps):
        if t > 0:
            lane = iota((rows, rows), 1)
            source = lane - lane % BEAMS + parents[t - 1 : t]
            pick = jnp.where(iota((rows, rows), 0) == source, 1.0, 0.0).T
            pick16 = pick.astype(BF16)
            keys = [dot(pick16, a).astype(BF16) for a in keys]
            vals = [dot(pick16, a).astype(BF16) for a in vals]
            sums = [exact_dot(pick, a) for a in sums]
        keys.append(k[t])
        vals.append(v[t])
        sums.append(f[t] + sums[-1] if t > 0 else f[t])
        asked = q[t].astype(F32)
        scores = []
        for key, total in zip(keys, sums):
            product = asked * key.astype(F32)
            high = product.astype(BF16)
            low = (product - high.astype(F32)).astype(BF16)
            scores.append((dot(high, same) + dot(low, same)) - total)
        best = functools.reduce(jnp.maximum, scores)
        weights = [jnp.exp(s - best) for s in scores]
        top_out[t] = best
        total_out[t] = functools.reduce(jnp.add, weights)
        numer_out[t] = functools.reduce(
            jnp.add, [w.astype(BF16).astype(F32) * a.astype(F32) for w, a in zip(weights, vals)]
        )


def group_kernel(
    groups, local, heads, request, fill, tokens_h, gain, wq, wk, wv, wf, bias, parents, keys_h, values_h, decay,
    att,
    tokens, wbuf, keys, values, dec, normed, q_req, q_step, k_new, v_new, f_new,
    table, table_in, loc_v, send, q_in, sent, arrived, s_numer, s_top, s_total, h_numer, h_top, h_total, final,
    loc, last, slot,
    lsem, msem, tsend, trecv, qsend, qrecv, rsend, rrecv,
):
    steps, rows, width = q_step.shape
    span = steps * BEAMS
    pages = keys.shape[0]
    owned = pages - SPILL
    size = width // heads
    blocks = width // 128
    me = lax.axis_index("group")
    loads = [
        pltpu.make_async_copy(a, b, lsem.at[i])
        for i, (a, b) in enumerate(
            (
                (tokens_h, tokens),
                (wq, wbuf.at[0]),
                (wk, wbuf.at[1]),
                (wv, wbuf.at[2]),
                (keys_h, keys),
                (values_h, values),
            )
        )
    ]
    for load in loads:
        load.start()
    barrier = pltpu.get_barrier_semaphore()

    def peer_of(d):
        return lax.rem(me + d, groups)

    def each_peer(body):
        def step(d, c):
            body(d)
            return c

        lax.fori_loop(1, groups, step, 0)

    each_peer(
        lambda d: pl.semaphore_signal(
            barrier, inc=1, device_id={"group": peer_of(d)}, device_id_type=MESH
        )
    )

    def remote(src, dst, ssem, rsem, d):
        return pltpu.make_async_remote_copy(
            src_ref=src,
            dst_ref=dst,
            send_sem=ssem,
            recv_sem=rsem,
            device_id={"group": peer_of(d)},
            device_id_type=MESH,
        )

    def table_copy(d, there):
        return remote(table, table_in.at[there], tsend.at[d], trecv.at[there], d)

    def query_copy(d, there):
        return remote(send.at[peer_of(d)], q_in.at[there], qsend.at[d], qrecv.at[there], d)

    def result_copy(peer, there):
        return pltpu.make_async_remote_copy(
            src_ref=sent.at[peer],
            dst_ref=arrived.at[there],
            send_sem=rsend.at[peer],
            recv_sem=rrecv.at[there],
            device_id={"group": peer},
            device_id_type=MESH,
        )

    lane = iota(table.shape, 1)
    heard = jnp.full(table.shape, -1, jnp.int32)
    for s in range(SPILL):
        heard = jnp.where(lane == s, request[owned + s], heard)
    table[...] = heard
    table_in[pl.ds(me, 1)] = jnp.full((1,) + table.shape, -1, jnp.int32)
    q_in[pl.ds(me, 1)] = jnp.zeros((1, span, width), BF16)
    loads[0].wait()

    def norm_step(t, c):
        normed[pl.ds(t * rows, rows)] = rms(tokens[t].astype(F32), gain[...]).astype(BF16)
        return c

    lax.fori_loop(0, steps, norm_step, 0)
    pl.semaphore_wait(barrier, groups - 1)
    each_peer(lambda d: table_copy(d, me).start())
    loads[1].wait()
    q = dot_nt(normed[...], wbuf[0]).astype(BF16).astype(F32) * size ** (-0.5)
    q_step[...] = q.astype(BF16).reshape(steps, rows, width)
    q_req[...] = (
        q.reshape(steps, local, BEAMS, width)
        .transpose(1, 0, 2, 3)
        .reshape(local, span, width)
        .astype(BF16)
    )
    each_peer(lambda d: table_copy(d, lax.rem(me + d, groups)).wait_recv())
    batch = 8
    flat = q_req[...].reshape(local * span, width)

    def select_batch(i, c):
        heard = table_in[pl.ds(i * batch, batch)]
        where = jnp.max(
            jnp.where(heard // local == me, heard - me * local, -1), axis=-1, keepdims=True
        )
        rows8 = table_in[pl.ds(i * batch, batch), 0, :]
        where8 = jnp.max(
            jnp.where(rows8 // local == me, rows8 - me * local, -1), axis=-1, keepdims=True
        )
        loc_v[pl.ds(pl.multiple_of(i * batch, batch), batch)] = jnp.broadcast_to(where8, (batch, 128))
        tall = jnp.concatenate([where] * (span // 8), axis=1)
        shape = (batch, span, local * span)
        hit = iota(shape, 2) - iota(shape, 1) == tall * span
        pick = jnp.where(hit, 1.0, 0.0).astype(BF16).reshape(batch * span, local * span)
        send[pl.ds(i * batch, batch)] = dot(pick, flat).astype(BF16).reshape(batch, span, width)
        return c

    lax.fori_loop(0, groups // batch, select_batch, 0)
    each_peer(lambda d: query_copy(d, me).start())
    to_scalar = pltpu.make_async_copy(loc_v, loc, msem.at[0])
    to_scalar.start()

    loads[2].wait()
    k_new[...] = dot_nt(normed[...], wbuf[1]).astype(BF16).reshape(steps, rows, width)
    loads[3].wait()
    v_new[...] = dot_nt(normed[...], wbuf[2]).astype(BF16).reshape(steps, rows, width)
    gate = jax.nn.log_sigmoid(dot_nt(normed[...], wf[...]) + bias[...])
    spread = jnp.where(iota((heads, width), 1) // size == iota((heads, width), 0), 1.0, 0.0)
    f_new[...] = exact_dot(gate, spread).reshape(steps, rows, width)
    dec[...] = decay[...].astype(F32)
    low = iota((span, 128), 1) < 64
    masks = jnp.concatenate([jnp.where(low, 1.0, 0.0), jnp.where(low, 0.0, 1.0)], axis=0).astype(BF16)

    def bias_of(page):
        inside = iota((1, 128), 1) < fill[page]
        return [jnp.where(inside, dec[h, pl.ds(page, 1), :], MASKED) for h in range(heads)]

    for r in range(local):
        last[r] = 0
    for s in range(groups):
        found = jnp.int32(0)
        for i in range(SPILL):
            found = jnp.where(request[owned + i] // local == s, i, found)
        slot[s] = found
    s_numer[0] = jnp.zeros((span, width), F32)
    s_total[0] = jnp.zeros((span, width), F32)
    s_top[0] = jnp.full((span, width), MASKED, F32)

    def chain(r, entry, numer, top, total):
        before = last[jnp.maximum(r, 0)]
        for j in range(blocks):
            cut = slice(128 * j, 128 * (j + 1))
            old = s_top[before, :, cut]
            best = jnp.maximum(old, top[j])
            keep = jnp.exp(old - best)
            add = jnp.exp(top[j] - best)
            s_numer[entry, :, cut] = s_numer[before, :, cut] * keep + numer[j] * add
            s_total[entry, :, cut] = s_total[before, :, cut] * keep + total[j] * add
            s_top[entry, :, cut] = best
        for i in range(local):
            last[i] = jnp.where(r == i, entry, last[i])

    loads[4].wait()
    loads[5].wait()
    unroll = 4

    def own_pages(i, c):
        found = []
        for u in range(unroll):
            page = i * unroll + u
            r = lax.rem(request[page], local)
            found.append(
                (r, page, page_partial(q_req[r], masks, keys.at[page], values.at[page], bias_of(page)))
            )
        for r, page, (numer, top, total, _, _) in found:
            chain(r, page + 1, numer, top, total)
        return c

    lax.fori_loop(0, owned // unroll, own_pages, 0)

    pair = 2

    def hosted(i, c):
        found = []
        for u in range(pair):
            d = i * pair + u
            source = lax.rem(me - d + groups, groups)

            @pl.when(d > 0)
            def _():
                remote(send.at[source], q_in.at[source], qsend.at[0], qrecv.at[source], 1).wait_recv()

        for u in range(pair):
            source = lax.rem(me - (i * pair + u) + groups, groups)
            page = owned + slot[source]
            found.append(
                (source, page_partial(q_in[source], masks, keys.at[page], values.at[page], bias_of(page)))
            )
        for source, (numer, _, _, tops, totals) in found:
            for j in range(blocks):
                sent[source, :, 128 * j : 128 * (j + 1)] = numer[j].astype(BF16)
            sent[source, :, width:] = pack_stats(tops, totals).astype(BF16)
        for u in range(pair):
            d = i * pair + u
            source = lax.rem(me - d + groups, groups)

            @pl.when(d > 0)
            def _():
                result_copy(source, me).start()

        return c

    lax.fori_loop(0, groups // pair, hosted, 0)
    history(q_step, k_new, v_new, f_new, parents, h_numer, h_top, h_total, heads)
    to_scalar.wait()
    shape = (STAT, 2 * width)
    row, col = iota(shape, 0), iota(shape, 1)
    second = jnp.where(col >= width, 1, 0)
    expand = (row // 8 // 3 == second) & (row % 8 == (col - second * width) // size)
    expand = jnp.where(expand, 1.0, 0.0).astype(BF16)

    def absorb(d, c):
        source = peer_of(d)
        result_copy(source, source).wait_recv()
        stats = dot(arrived[source, :, width:], expand)
        cuts = [slice(128 * j, 128 * (j + 1)) for j in range(blocks)]
        numer = [arrived[source, :, cut].astype(F32) for cut in cuts]
        top = [stats[:, cut] for cut in cuts]
        total = [stats[:, width + cut.start : width + cut.stop] for cut in cuts]
        chain(loc[source, 0], owned + d, numer, top, total)
        return c

    lax.fori_loop(1, groups, absorb, 0)

    for r in range(local):
        cut = slice(r * BEAMS, (r + 1) * BEAMS)
        entry = last[r]
        shape = (steps, BEAMS, width)
        p_top = s_top[entry].reshape(shape)
        best = jnp.maximum(p_top, h_top[:, cut])
        p_scale = jnp.exp(p_top - best)
        h_scale = jnp.exp(h_top[:, cut] - best)
        whole = s_total[entry].reshape(shape) * p_scale + h_total[:, cut] * h_scale
        mixed = s_numer[entry].reshape(shape) * p_scale + h_numer[:, cut] * h_scale
        final[:, cut] = mixed / whole
    att[...] = final[...].astype(BF16)

    def finish(d):
        table_copy(d, me).wait_send()
        query_copy(d, me).wait_send()
        result_copy(peer_of(d), me).wait_send()

    each_peer(finish)


def tail_kernel(
    att, tokens, gain, wo_h, wg_h, wu_h, wd_h, out,
    wo, wg, wu, wd, keep, resid, normed, acc,
    a_tx, a_rx, b_tx, b_rx, c_tx, c_rx, d_tx, d_rx,
    wsem, sems_s, sems_r,
):
    steps, rows, model = out.shape
    half = rows // 2
    me = lax.axis_index("head")
    core = lax.rem(me, 2)
    sibling = {"head": me + 1 - 2 * core}
    chip = me // 2
    across = {"head": core + 2 * (1 - chip)}
    mine = pl.ds(pl.multiple_of(core * half, half), half)
    theirs = pl.ds(pl.multiple_of((1 - core) * half, half), half)
    loads = [
        pltpu.make_async_copy(a, b, wsem.at[i])
        for i, (a, b) in enumerate(((wo_h, wo), (wg_h, wg), (wu_h, wu), (wd_h, wd)))
    ]
    for load in loads:
        load.start()
    greet((sibling, across))

    def remote(kind, t, src, dst, device):
        return pltpu.make_async_remote_copy(
            src_ref=src,
            dst_ref=dst,
            send_sem=sems_s.at[kind, t],
            recv_sem=sems_r.at[kind, t],
            device_id=device,
            device_id_type=MESH,
        )

    copy_a = lambda t: remote(0, t, a_tx.at[t], a_rx.at[t], sibling)
    copy_b = lambda t: remote(1, t, b_tx.at[t], b_rx.at[t], across)
    copy_n = lambda t: remote(2, t, normed.at[t, mine], normed.at[t, mine], sibling)
    copy_n_in = lambda t: remote(2, t, normed.at[t, theirs], normed.at[t, theirs], sibling)
    copy_c = lambda t: remote(3, t, c_tx.at[t], c_rx.at[t], sibling)
    copy_d = lambda t: remote(4, t, d_tx.at[t], d_rx.at[t], across)
    copy_o = lambda t: remote(5, t, out.at[t, mine], out.at[t, mine], sibling)
    copy_o_in = lambda t: remote(5, t, out.at[t, theirs], out.at[t, theirs], sibling)

    loads[0].wait()

    def project(t, c):
        acc[...] = dot(att[t], wo[...])
        keep[t] = acc[mine]
        a_tx[t] = acc[theirs].astype(BF16)
        copy_a(t).start()
        return c

    lax.fori_loop(0, steps, project, 0)

    def cross(t, c):
        copy_a(t).wait_recv()
        b_tx[t] = (keep[t] + a_rx[t].astype(F32)).astype(BF16)
        copy_b(t).start()
        return c

    lax.fori_loop(0, steps, cross, 0)
    for load in loads[1:]:
        load.wait()

    def down_cross(t):
        copy_c(t).wait_recv()
        d_tx[t] = (keep[t] + c_rx[t].astype(F32)).astype(BF16)
        copy_d(t).start()

    def feed(t, c):
        copy_b(t).wait_recv()
        res = tokens[t, mine].astype(F32) + (b_tx[t].astype(F32) + b_rx[t].astype(F32))
        resid[t] = res
        normed[t, mine] = rms(res, gain[...]).astype(BF16)
        copy_n(t).start()

        @pl.when(t > 0)
        def _():
            down_cross(t - 1)

        copy_n_in(t).wait_recv()
        x = normed[t]
        gate = dot(x, wg[...])
        up = dot(x, wu[...])
        hidden = (gate / (1.0 + jnp.exp(-gate)) * up).astype(BF16)
        acc[...] = dot(hidden, wd[...])
        keep[t] = acc[mine]
        c_tx[t] = acc[theirs].astype(BF16)
        copy_c(t).start()
        return c

    lax.fori_loop(0, steps, feed, 0)
    down_cross(steps - 1)

    def close(t, c):
        copy_d(t).wait_recv()
        total = resid[t] + (d_tx[t].astype(F32) + d_rx[t].astype(F32))
        out[t, mine] = total.astype(BF16)
        copy_o(t).start()
        return c

    lax.fori_loop(0, steps, close, 0)

    def finish(t, c):
        copy_o_in(t).wait_recv()
        copy_a(t).wait_send()
        copy_b(t).wait_send()
        copy_n(t).wait_send()
        copy_c(t).wait_send()
        copy_d(t).wait_send()
        copy_o(t).wait_send()
        return c

    lax.fori_loop(0, steps, finish, 0)


VM = pl.BlockSpec(memory_space=pltpu.VMEM)
SM = pl.BlockSpec(memory_space=pltpu.SMEM)
HB = pl.BlockSpec(memory_space=pl.ANY)
DMA = pltpu.SemaphoreType.DMA
LIMIT = 60 << 20


def params(**kw):
    return pltpu.CompilerParams(vmem_limit_bytes=LIMIT, **kw)


def shards(
    tokens, parents, page_request, page_fill, keys_pool, values_pool, decay_pool, gain_attn,
    w_query, w_key, w_value, w_forget, forget_bias, w_out, gain_ffn, w_gate, w_up, w_down,
):
    steps, rows, model = tokens.shape
    heads = w_forget.shape[1]
    width = w_query.shape[0]
    local = rows // BEAMS
    span = steps * BEAMS
    groups = lax.axis_size("group")
    pages = page_request.shape[0]
    ff = w_gate.shape[1]
    sds = jax.ShapeDtypeStruct
    block = (steps, rows, width)
    chain = (pages - SPILL + groups, span, width)
    attended = pl.pallas_call(
        functools.partial(group_kernel, groups, local, heads),
        out_shape=sds(block, BF16),
        in_specs=[SM, SM, HB, VM, HB, HB, HB, VM, VM, VM, HB, HB, VM],
        out_specs=VM,
        scratch_shapes=[
            pltpu.VMEM(tokens.shape, BF16),
            pltpu.VMEM((3, width, model), BF16),
            pltpu.VMEM(keys_pool.shape, BF16),
            pltpu.VMEM(values_pool.shape, BF16),
            pltpu.VMEM((heads, pages, 128), F32),
            pltpu.VMEM((steps * rows, model), BF16),
            pltpu.VMEM((local, span, width), BF16),
            pltpu.VMEM(block, BF16),
            pltpu.VMEM(block, BF16),
            pltpu.VMEM(block, BF16),
            pltpu.VMEM(block, F32),
            pltpu.VMEM((8, 128), jnp.int32),
            pltpu.VMEM((groups, 8, 128), jnp.int32),
            pltpu.VMEM((groups, 128), jnp.int32),
            pltpu.VMEM((groups, span, width), BF16),
            pltpu.VMEM((groups, span, width), BF16),
            pltpu.VMEM((groups, span, width + STAT), BF16),
            pltpu.VMEM((groups, span, width + STAT), BF16),
        ]
        + [pltpu.VMEM(chain, F32)] * 3
        + [pltpu.VMEM(block, F32)] * 4
        + [
            pltpu.SMEM((groups, 128), jnp.int32),
            pltpu.SMEM((local,), jnp.int32),
            pltpu.SMEM((groups,), jnp.int32),
            DMA((6,)),
            DMA((1,)),
        ]
        + [DMA((groups,))] * 6,
        compiler_params=params(collective_id=0, has_side_effects=True),
        name="group",
    )(
        page_request, page_fill, tokens, gain_attn, w_query, w_key, w_value, w_forget.T,
        forget_bias[None], parents, keys_pool, values_pool, decay_pool.transpose(1, 0, 2),
    )

    half = (steps, rows // 2, model)
    return pl.pallas_call(
        tail_kernel,
        out_shape=sds((steps, rows, model), BF16),
        in_specs=[VM, VM, VM, HB, HB, HB, HB],
        out_specs=VM,
        scratch_shapes=[
            pltpu.VMEM((width, model), BF16),
            pltpu.VMEM((model, ff), BF16),
            pltpu.VMEM((model, ff), BF16),
            pltpu.VMEM((ff, model), BF16),
            pltpu.VMEM(half, F32),
            pltpu.VMEM(half, F32),
            pltpu.VMEM((steps, rows, model), BF16),
            pltpu.VMEM((rows, model), F32),
        ]
        + [pltpu.VMEM(half, BF16)] * 8
        + [DMA((4,)), DMA((6, steps)), DMA((6, steps))],
        compiler_params=params(collective_id=2, has_side_effects=True),
        name="tail",
    )(attended, tokens, gain_ffn, w_out, w_gate, w_up, w_down)


def solution(mesh):
    return jax.shard_map(
        shards,
        mesh=mesh,
        in_specs=(
            P(None, "group", None),
            P(None, "group"),
            P("group"),
            P("group"),
            P("group", "head", None),
            P("group", "head", None),
            P("group", "head", None),
            P(),
            P("head", None),
            P("head", None),
            P("head", None),
            P(None, "head"),
            P("head"),
            P("head", None),
            P(),
            P(None, "head"),
            P(None, "head"),
            P("head", None),
        ),
        out_specs=P(None, "group", None),
        check_vma=False,
    )
```

time: 148 us -> 97 us (0.66)
  Pallas kernels: 136 us -> 94.1 us
  local copies, waits for them, and re-layouts: 9.68 us -> 2.65 us
  other arithmetic: 2.01 us -> 0 us
    pallas_call x4 -> x1, Pallas kernels: 92.5 us -> 49 us  [shards(): pl.pallas_call(functools.partial(group_kernel, groups, local, heads), out...]
    unnamed x7 -> x1, local copies, waits for them, and re-layouts: 5.02 us -> 2.65 us
    slice x1 -> x0, local copies, waits for them, and re-layouts: 2.18 us -> none  [shards(): loc[:, 0, 0]]
    pallas_call x1, Pallas kernels: 43.1 us -> 45.2 us  [shards(): pl.pallas_call(tail_kernel, out_shape=sds((steps, rows, model), BF16), in...]
    another operation x2 -> x0, other arithmetic: 2.01 us -> none
    broadcast_in_dim x2 -> x0, local copies, waits for them, and re-layouts: 1.89 us -> none  [the longest x1 1.29 us: shards(): gain_attn[None]]
where the time goes in v2:
time: 97 us; the launch traced here: 96.8 us
  Pallas kernels  94.1 us (97%)
  local copies, waits for them, and re-layouts  2.65 us (3%)
    pallas_call x1, Pallas kernels, shards(): pl.pallas_call(functools.partial(group_kernel, groups, local, heads), out...  49 us
    pallas_call x1, Pallas kernels, shards(): pl.pallas_call(tail_kernel, out_shape=sds((steps, rows, model), BF16), in...  45.2 us
    unnamed x1, local copies, waits for them, and re-layouts  2.65 us

profile of v2, /device:TPU:1, one launch (start us, length us, event | category | flops | bytes accessed | tf_op | source)
XLA Modules:
  0.0 96.8 jit_solution(16824024093344921875)
XLA Ops:
  0.0 49.0 %group.1.att = bf16[4,128,384]{2,1,0:T(8,128)(2,1)} custom-call(s32[48]{0:T(128)} %request.1, s32[48]{0:T(128)} %fill.1, bf16[4,128,1536]{2,1,0:T(8,128)(2,1)} %tokens.1, f32[1536]{0:T(1024)} %gain.2, bf16[384,1536]{1,0:T(8,128)(2,1)} %wq.1, bf16[384,1536]{1,0:T(8,128)(2,1)} %wk.1, bf16[384,1536]{1,0:T(8,128)(2,1)} %wv.1, bf16[6,1536]{1,0:T(8,128)(2,1)} %bitcast.4, ...), custom_call_target="tpu_custom_call" | custom-call | tf_op jit(solution)/shard_map/group/pallas_call | solution.py:534
  49.0 45.2 %tail.1 = bf16[4,128,1536]{2,1,0:T(8,128)(2,1)} custom-call(bf16[4,128,384]{2,1,0:T(8,128)(2,1)} %group.1.att, bf16[4,128,1536]{2,1,0:T(8,128)(2,1)} %tokens.1, f32[1536]{0:T(1024)} %gain.3, bf16[384,1536]{1,0:T(8,128)(2,1)} %wo_h.1, bf16[1536,1024]{1,0:T(8,128)(2,1)} %wg_h.1, bf16[1536,1024]{1,0:T(8,128)(2,1)} %wu_h.1, bf16[1024,1536]{1,0:T(8,128)(2,1)} %wd_h.1), custom_call_target="tpu_custom_call" | custom-call | tf_op jit(solution)/shard_map/tail/pallas_call | solution.py:577
  94.2 2.7 %copy.20 = bf16[4,128,1536]{2,1,0:T(8,128)(2,1)} copy(bf16[4,128,1536]{2,1,0:T(8,128)(2,1)} %tail.1) | data formatting | bytes 3145728

commit v3 on v2

--- a/solution.py
+++ b/solution.py
@@ -36,27 +36,6 @@
 
 def iota(shape, dim):
     return lax.broadcasted_iota(jnp.int32, shape, dim)
-
-
-def greet(peers):
-    barrier = pltpu.get_barrier_semaphore()
-    count = 0
-    for peer in peers:
-        pl.semaphore_signal(barrier, inc=1, device_id=peer, device_id_type=MESH)
-        count += 1
-    pl.semaphore_wait(barrier, count)
-
-
-def greet_group(groups, me):
-    barrier = pltpu.get_barrier_semaphore()
-
-    def signal(d, c):
-        peer = lax.rem(me + d, groups)
-        pl.semaphore_signal(barrier, inc=1, device_id={"group": peer}, device_id_type=MESH)
-        return c
-
-    lax.fori_loop(1, groups, signal, 0)
-    pl.semaphore_wait(barrier, groups - 1)
 
 
 def page_partial(q, masks, keys, values, bias):
@@ -134,11 +113,15 @@
 
 def group_kernel(
     groups, local, heads, request, fill, tokens_h, gain, wq, wk, wv, wf, bias, parents, keys_h, values_h, decay,
-    att,
-    tokens, wbuf, keys, values, dec, normed, q_req, q_step, k_new, v_new, f_new,
+    wo_h, gain_ffn, wg_h, wu_h, wd_h,
+    out,
+    att, tokens, wbuf, keys, values, dec, normed, q_req, q_step, k_new, v_new, f_new,
     table, table_in, loc_v, send, q_in, sent, arrived, s_numer, s_top, s_total, h_numer, h_top, h_total, final,
     loc, last, slot,
     lsem, msem, tsend, trecv, qsend, qrecv, rsend, rrecv,
+    wo, wg, wu, wd, keep, residual, normed_ffn, acc,
+    a_tx, a_rx, b_tx, b_rx, c_tx, c_rx, d_tx, d_rx,
+    wsem, sems_s, sems_r,
 ):
     steps, rows, width = q_step.shape
     span = steps * BEAMS
@@ -147,6 +130,15 @@
     size = width // heads
     blocks = width // 128
     me = lax.axis_index("group")
+    half = rows // 2
+    head = lax.axis_index("head")
+    core = lax.rem(head, 2)
+    sibling = {"head": head + 1 - 2 * core}
+    across = {"head": core + 2 * (1 - head // 2)}
+    wloads = [
+        pltpu.make_async_copy(a, b, wsem.at[i])
+        for i, (a, b) in enumerate(((wo_h, wo), (wg_h, wg), (wu_h, wu), (wd_h, wd)))
+    ]
     loads = [
         pltpu.make_async_copy(a, b, lsem.at[i])
         for i, (a, b) in enumerate(
@@ -160,7 +152,7 @@
             )
         )
     ]
-    for load in loads:
+    for load in loads[:2]:
         load.start()
     barrier = pltpu.get_barrier_semaphore()
 
@@ -179,6 +171,9 @@
             barrier, inc=1, device_id={"group": peer_of(d)}, device_id_type=MESH
         )
     )
+
+    for other in (sibling, across):
+        pl.semaphore_signal(barrier, inc=1, device_id=other, device_id_type=MESH)
 
     def remote(src, dst, ssem, rsem, d):
         return pltpu.make_async_remote_copy(
@@ -213,6 +208,8 @@
     table[...] = heard
     table_in[pl.ds(me, 1)] = jnp.full((1,) + table.shape, -1, jnp.int32)
     q_in[pl.ds(me, 1)] = jnp.zeros((1, span, width), BF16)
+    pl.semaphore_wait(barrier, groups + 1)
+    each_peer(lambda d: table_copy(d, me).start())
     loads[0].wait()
 
     def norm_step(t, c):
@@ -220,42 +217,35 @@
         return c
 
     lax.fori_loop(0, steps, norm_step, 0)
-    pl.semaphore_wait(barrier, groups - 1)
-    each_peer(lambda d: table_copy(d, me).start())
+    for load in loads[2:] + wloads:
+        load.start()
+    each_peer(lambda d: table_copy(d, lax.rem(me + d, groups)).wait_recv())
+    batch = 8
+    for i in range(groups // batch):
+        heard = table_in[i * batch : (i + 1) * batch, 0, :]
+        where = jnp.max(
+            jnp.where(heard // local == me, heard - me * local, -1), axis=-1, keepdims=True
+        )
+        loc_v[i * batch : (i + 1) * batch] = jnp.broadcast_to(where, (batch, 128))
+    to_scalar = pltpu.make_async_copy(loc_v, loc, msem.at[0])
+    to_scalar.start()
     loads[1].wait()
     q = dot_nt(normed[...], wbuf[0]).astype(BF16).astype(F32) * size ** (-0.5)
-    q_step[...] = q.astype(BF16).reshape(steps, rows, width)
     q_req[...] = (
         q.reshape(steps, local, BEAMS, width)
         .transpose(1, 0, 2, 3)
         .reshape(local, span, width)
         .astype(BF16)
     )
-    each_peer(lambda d: table_copy(d, lax.rem(me + d, groups)).wait_recv())
-    batch = 8
-    flat = q_req[...].reshape(local * span, width)
-
-    def select_batch(i, c):
-        heard = table_in[pl.ds(i * batch, batch)]
-        where = jnp.max(
-            jnp.where(heard // local == me, heard - me * local, -1), axis=-1, keepdims=True
-        )
-        rows8 = table_in[pl.ds(i * batch, batch), 0, :]
-        where8 = jnp.max(
-            jnp.where(rows8 // local == me, rows8 - me * local, -1), axis=-1, keepdims=True
-        )
-        loc_v[pl.ds(pl.multiple_of(i * batch, batch), batch)] = jnp.broadcast_to(where8, (batch, 128))
-        tall = jnp.concatenate([where] * (span // 8), axis=1)
-        shape = (batch, span, local * span)
-        hit = iota(shape, 2) - iota(shape, 1) == tall * span
-        pick = jnp.where(hit, 1.0, 0.0).astype(BF16).reshape(batch * span, local * span)
-        send[pl.ds(i * batch, batch)] = dot(pick, flat).astype(BF16).reshape(batch, span, width)
-        return c
-
-    lax.fori_loop(0, groups // batch, select_batch, 0)
-    each_peer(lambda d: query_copy(d, me).start())
-    to_scalar = pltpu.make_async_copy(loc_v, loc, msem.at[0])
-    to_scalar.start()
+    to_scalar.wait()
+
+    def send_query(d):
+        peer = peer_of(d)
+        send[peer] = q_req[jnp.maximum(loc[peer, 0], 0)]
+        query_copy(d, me).start()
+
+    each_peer(send_query)
+    q_step[...] = q.astype(BF16).reshape(steps, rows, width)
 
     loads[2].wait()
     k_new[...] = dot_nt(normed[...], wbuf[1]).astype(BF16).reshape(steps, rows, width)
@@ -299,22 +289,7 @@
 
     loads[4].wait()
     loads[5].wait()
-    unroll = 4
-
-    def own_pages(i, c):
-        found = []
-        for u in range(unroll):
-            page = i * unroll + u
-            r = lax.rem(request[page], local)
-            found.append(
-                (r, page, page_partial(q_req[r], masks, keys.at[page], values.at[page], bias_of(page)))
-            )
-        for r, page, (numer, top, total, _, _) in found:
-            chain(r, page + 1, numer, top, total)
-        return c
-
-    lax.fori_loop(0, owned // unroll, own_pages, 0)
-
+    history(q_step, k_new, v_new, f_new, parents, h_numer, h_top, h_total, heads)
     pair = 2
 
     def hosted(i, c):
@@ -348,8 +323,22 @@
         return c
 
     lax.fori_loop(0, groups // pair, hosted, 0)
-    history(q_step, k_new, v_new, f_new, parents, h_numer, h_top, h_total, heads)
-    to_scalar.wait()
+    unroll = 4
+
+    def own_pages(i, c):
+        found = []
+        for u in range(unroll):
+            page = i * unroll + u
+            r = lax.rem(request[page], local)
+            found.append(
+                (r, page, page_partial(q_req[r], masks, keys.at[page], values.at[page], bias_of(page)))
+            )
+        for r, page, (numer, top, total, _, _) in found:
+            chain(r, page + 1, numer, top, total)
+        return c
+
+    lax.fori_loop(0, owned // unroll, own_pages, 0)
+
     shape = (STAT, 2 * width)
     row, col = iota(shape, 0), iota(shape, 1)
     second = jnp.where(col >= width, 1, 0)
@@ -389,31 +378,9 @@
 
     each_peer(finish)
 
-
-def tail_kernel(
-    att, tokens, gain, wo_h, wg_h, wu_h, wd_h, out,
-    wo, wg, wu, wd, keep, resid, normed, acc,
-    a_tx, a_rx, b_tx, b_rx, c_tx, c_rx, d_tx, d_rx,
-    wsem, sems_s, sems_r,
-):
-    steps, rows, model = out.shape
-    half = rows // 2
-    me = lax.axis_index("head")
-    core = lax.rem(me, 2)
-    sibling = {"head": me + 1 - 2 * core}
-    chip = me // 2
-    across = {"head": core + 2 * (1 - chip)}
     mine = pl.ds(pl.multiple_of(core * half, half), half)
     theirs = pl.ds(pl.multiple_of((1 - core) * half, half), half)
-    loads = [
-        pltpu.make_async_copy(a, b, wsem.at[i])
-        for i, (a, b) in enumerate(((wo_h, wo), (wg_h, wg), (wu_h, wu), (wd_h, wd)))
-    ]
-    for load in loads:
-        load.start()
-    greet((sibling, across))
-
-    def remote(kind, t, src, dst, device):
+    def pair_copy(kind, t, src, dst, device):
         return pltpu.make_async_remote_copy(
             src_ref=src,
             dst_ref=dst,
@@ -423,34 +390,41 @@
             device_id_type=MESH,
         )
 
-    copy_a = lambda t: remote(0, t, a_tx.at[t], a_rx.at[t], sibling)
-    copy_b = lambda t: remote(1, t, b_tx.at[t], b_rx.at[t], across)
-    copy_n = lambda t: remote(2, t, normed.at[t, mine], normed.at[t, mine], sibling)
-    copy_n_in = lambda t: remote(2, t, normed.at[t, theirs], normed.at[t, theirs], sibling)
-    copy_c = lambda t: remote(3, t, c_tx.at[t], c_rx.at[t], sibling)
-    copy_d = lambda t: remote(4, t, d_tx.at[t], d_rx.at[t], across)
-    copy_o = lambda t: remote(5, t, out.at[t, mine], out.at[t, mine], sibling)
-    copy_o_in = lambda t: remote(5, t, out.at[t, theirs], out.at[t, theirs], sibling)
-
-    loads[0].wait()
-
-    def project(t, c):
+    copy_a = lambda t: pair_copy(0, t, a_tx.at[t], a_rx.at[t], sibling)
+    copy_b = lambda t: pair_copy(1, t, b_tx.at[t], b_rx.at[t], across)
+    copy_n = lambda t: pair_copy(2, t, normed_ffn.at[t, mine], normed_ffn.at[t, mine], sibling)
+    copy_n_in = lambda t: pair_copy(2, t, normed_ffn.at[t, theirs], normed_ffn.at[t, theirs], sibling)
+    copy_c = lambda t: pair_copy(3, t, c_tx.at[t], c_rx.at[t], sibling)
+    copy_d = lambda t: pair_copy(4, t, d_tx.at[t], d_rx.at[t], across)
+    copy_o = lambda t: pair_copy(5, t, out.at[t, mine], out.at[t, mine], sibling)
+    copy_o_in = lambda t: pair_copy(5, t, out.at[t, theirs], out.at[t, theirs], sibling)
+
+    wloads[0].wait()
+
+    def project(t):
         acc[...] = dot(att[t], wo[...])
         keep[t] = acc[mine]
         a_tx[t] = acc[theirs].astype(BF16)
         copy_a(t).start()
-        return c
-
-    lax.fori_loop(0, steps, project, 0)
-
-    def cross(t, c):
+
+    def cross(t):
         copy_a(t).wait_recv()
         b_tx[t] = (keep[t] + a_rx[t].astype(F32)).astype(BF16)
         copy_b(t).start()
-        return c
-
-    lax.fori_loop(0, steps, cross, 0)
-    for load in loads[1:]:
+
+    def lead(t, c):
+        @pl.when(t < steps)
+        def _():
+            project(t)
+
+        @pl.when(t > 0)
+        def _():
+            cross(t - 1)
+
+        return c
+
+    lax.fori_loop(0, steps + 1, lead, 0)
+    for load in wloads[1:]:
         load.wait()
 
     def down_cross(t):
@@ -461,8 +435,8 @@
     def feed(t, c):
         copy_b(t).wait_recv()
         res = tokens[t, mine].astype(F32) + (b_tx[t].astype(F32) + b_rx[t].astype(F32))
-        resid[t] = res
-        normed[t, mine] = rms(res, gain[...]).astype(BF16)
+        residual[t] = res
+        normed_ffn[t, mine] = rms(res, gain_ffn[...]).astype(BF16)
         copy_n(t).start()
 
         @pl.when(t > 0)
@@ -470,7 +444,7 @@
             down_cross(t - 1)
 
         copy_n_in(t).wait_recv()
-        x = normed[t]
+        x = normed_ffn[t]
         gate = dot(x, wg[...])
         up = dot(x, wu[...])
         hidden = (gate / (1.0 + jnp.exp(-gate)) * up).astype(BF16)
@@ -483,16 +457,16 @@
     lax.fori_loop(0, steps, feed, 0)
     down_cross(steps - 1)
 
-    def close(t, c):
+    def emit(t, c):
         copy_d(t).wait_recv()
-        total = resid[t] + (d_tx[t].astype(F32) + d_rx[t].astype(F32))
+        total = residual[t] + (d_tx[t].astype(F32) + d_rx[t].astype(F32))
         out[t, mine] = total.astype(BF16)
         copy_o(t).start()
         return c
 
-    lax.fori_loop(0, steps, close, 0)
-
-    def finish(t, c):
+    lax.fori_loop(0, steps, emit, 0)
+
+    def settle(t, c):
         copy_o_in(t).wait_recv()
         copy_a(t).wait_send()
         copy_b(t).wait_send()
@@ -502,7 +476,7 @@
         copy_o(t).wait_send()
         return c
 
-    lax.fori_loop(0, steps, finish, 0)
+    lax.fori_loop(0, steps, settle, 0)
 
 
 VM = pl.BlockSpec(memory_space=pltpu.VMEM)
@@ -531,12 +505,14 @@
     sds = jax.ShapeDtypeStruct
     block = (steps, rows, width)
     chain = (pages - SPILL + groups, span, width)
-    attended = pl.pallas_call(
+    half = (steps, rows // 2, model)
+    return pl.pallas_call(
         functools.partial(group_kernel, groups, local, heads),
-        out_shape=sds(block, BF16),
-        in_specs=[SM, SM, HB, VM, HB, HB, HB, VM, VM, VM, HB, HB, VM],
+        out_shape=sds(tokens.shape, BF16),
+        in_specs=[SM, SM, HB, VM, HB, HB, HB, VM, VM, VM, HB, HB, VM, HB, VM, HB, HB, HB],
         out_specs=VM,
         scratch_shapes=[
+            pltpu.VMEM(block, BF16),
             pltpu.VMEM(tokens.shape, BF16),
             pltpu.VMEM((3, width, model), BF16),
             pltpu.VMEM(keys_pool.shape, BF16),
@@ -565,35 +541,26 @@
             DMA((6,)),
             DMA((1,)),
         ]
-        + [DMA((groups,))] * 6,
-        compiler_params=params(collective_id=0, has_side_effects=True),
-        name="group",
-    )(
-        page_request, page_fill, tokens, gain_attn, w_query, w_key, w_value, w_forget.T,
-        forget_bias[None], parents, keys_pool, values_pool, decay_pool.transpose(1, 0, 2),
-    )
-
-    half = (steps, rows // 2, model)
-    return pl.pallas_call(
-        tail_kernel,
-        out_shape=sds((steps, rows, model), BF16),
-        in_specs=[VM, VM, VM, HB, HB, HB, HB],
-        out_specs=VM,
-        scratch_shapes=[
+        + [DMA((groups,))] * 6
+        + [
             pltpu.VMEM((width, model), BF16),
             pltpu.VMEM((model, ff), BF16),
             pltpu.VMEM((model, ff), BF16),
             pltpu.VMEM((ff, model), BF16),
             pltpu.VMEM(half, F32),
             pltpu.VMEM(half, F32),
-            pltpu.VMEM((steps, rows, model), BF16),
+            pltpu.VMEM(tokens.shape, BF16),
             pltpu.VMEM((rows, model), F32),
         ]
         + [pltpu.VMEM(half, BF16)] * 8
         + [DMA((4,)), DMA((6, steps)), DMA((6, steps))],
-        compiler_params=params(collective_id=2, has_side_effects=True),
-        name="tail",
-    )(attended, tokens, gain_ffn, w_out, w_gate, w_up, w_down)
+        compiler_params=params(collective_id=0, has_side_effects=True),
+        name="layer",
+    )(
+        page_request, page_fill, tokens, gain_attn, w_query, w_key, w_value, w_forget.T,
+        forget_bias[None], parents, keys_pool, values_pool, decay_pool.transpose(1, 0, 2),
+        w_out, gain_ffn, w_gate, w_up, w_down,
+    )
 
 
 def solution(mesh):

time: 97 us -> 89.9 us (0.927)
  Pallas kernels: 94.1 us -> 87.1 us
    pallas_call x1 -> x0, Pallas kernels: 45.2 us -> none  [shards(): pl.pallas_call(tail_kernel, out_shape=sds((steps, rows, model), BF16), in...]
    pallas_call x1, Pallas kernels: 49 us -> 87.1 us  [shards(): pl.pallas_call(functools.partial(group_kernel, groups, local, heads), out...]
where the time goes in v3:
time: 89.9 us; the launch traced here: 89.8 us
  Pallas kernels  87.1 us (97%)
  local copies, waits for them, and re-layouts  2.65 us (3%)
    pallas_call x1, Pallas kernels, shards(): pl.pallas_call(functools.partial(group_kernel, groups, local, heads), out...  87.1 us
    unnamed x1, local copies, waits for them, and re-layouts  2.65 us

profile of v3, /device:TPU:1, one launch (start us, length us, event | category | flops | bytes accessed | tf_op | source)
XLA Modules:
  0.0 89.8 jit_solution(7491549238834852705)
XLA Ops:
  0.0 87.1 %layer.1 = bf16[4,128,1536]{2,1,0:T(8,128)(2,1)} custom-call(s32[48]{0:T(128)} %request.1, s32[48]{0:T(128)} %fill.1, bf16[4,128,1536]{2,1,0:T(8,128)(2,1)} %tokens_h.1, f32[1536]{0:T(1024)} %gain.1, bf16[384,1536]{1,0:T(8,128)(2,1)} %wq.1, bf16[384,1536]{1,0:T(8,128)(2,1)} %wk.1, bf16[384,1536]{1,0:T(8,128)(2,1)} %wv.1, bf16[6,1536]{1,0:T(8,128)(2,1)} %bitcast.4, ...), custom_call_target="tpu_custom_call" | custom-call | tf_op jit(solution)/shard_map/layer/pallas_call | solution.py:509
  87.1 2.7 %copy.20 = bf16[4,128,1536]{2,1,0:T(8,128)(2,1)} copy(bf16[4,128,1536]{2,1,0:T(8,128)(2,1)} %layer.1) | data formatting | bytes 3145728

commit v4 on v3

--- a/solution.py
+++ b/solution.py
@@ -36,6 +36,10 @@
 
 def iota(shape, dim):
     return lax.broadcasted_iota(jnp.int32, shape, dim)
+
+
+def turn(values):
+    return values.astype(F32).T.astype(BF16)
 
 
 def page_partial(q, masks, keys, values, bias):
@@ -50,7 +54,7 @@
         best = jnp.max(scores, axis=-1, keepdims=True)
         weight = jnp.exp(scores - best)
         whole = jnp.sum(weight, axis=-1, keepdims=True)
-        out = dot(weight.astype(BF16), values[cut].astype(F32).T.astype(BF16))
+        out = dot(weight.astype(BF16), values[:, cut])
         numer.append(jnp.where(low, out[:span], out[span:]))
         best = jnp.broadcast_to(best, (2 * span, 128))
         whole = jnp.broadcast_to(whole, (2 * span, 128))
@@ -61,20 +65,27 @@
     return numer, top, total, tops, totals
 
 
+def stat_lanes(shape, dim, heads):
+    lane = iota(shape, dim)
+    place = lane % 32
+    return lane // 32, place % heads, place // heads
+
+
 def pack_stats(tops, totals):
-    span = tops[0].shape[0]
-    lane = iota((span, STAT), 1)
-    head, kind = lane % 8, lane // 8
-    value = jnp.zeros((span, STAT), F32)
-    for h, (a, b) in enumerate(zip(tops, totals)):
-        value = jnp.where(head == h, jnp.where(kind < 3, a, b), value)
+    heads = len(tops)
+    quarter = tops[0].shape[0] // 4
+    group, head, part = stat_lanes((quarter, STAT), 1, heads)
+    value = jnp.zeros((quarter, STAT), F32)
+    for g in range(4):
+        cut = slice(g * quarter, (g + 1) * quarter)
+        for h in range(heads):
+            both = jnp.where(part < 3, tops[h][cut], totals[h][cut])
+            value = jnp.where((group == g) & (head == h), both, value)
     first = value.astype(BF16).astype(F32)
     rest = value - first
     second = rest.astype(BF16).astype(F32)
-    third = rest - second
-    pick = jnp.where(kind < 3, kind, kind - 3)
-    out = jnp.where(pick == 0, first, jnp.where(pick == 1, second, third))
-    return jnp.where(kind < 6, out, 0.0)
+    out = jnp.where(part % 3 == 0, first, jnp.where(part % 3 == 1, second, rest - second))
+    return jnp.where(part < 5, out, 0.0)
 
 
 def history(q, k, v, f, parents, numer_out, top_out, total_out, heads):
@@ -114,14 +125,15 @@
 def group_kernel(
     groups, local, heads, request, fill, tokens_h, gain, wq, wk, wv, wf, bias, parents, keys_h, values_h, decay,
     wo_h, gain_ffn, wg_h, wu_h, wd_h,
-    out,
-    att, tokens, wbuf, keys, values, dec, normed, q_req, q_step, k_new, v_new, f_new,
+    result,
+    out, att, tokens, wbuf, keys, values, dec, normed, q_req, q_step, k_new, v_new, f_new,
     table, table_in, loc_v, send, q_in, sent, arrived, s_numer, s_top, s_total, h_numer, h_top, h_total, final,
+    turned,
     loc, last, slot,
     lsem, msem, tsend, trecv, qsend, qrecv, rsend, rrecv,
-    wo, wg, wu, wd, keep, residual, normed_ffn, acc,
+    wo, wg, wu, wd, keep, residual, acc,
     a_tx, a_rx, b_tx, b_rx, c_tx, c_rx, d_tx, d_rx,
-    wsem, sems_s, sems_r,
+    wsem, osem, sems_s, sems_r,
 ):
     steps, rows, width = q_step.shape
     span = steps * BEAMS
@@ -208,12 +220,13 @@
     table[...] = heard
     table_in[pl.ds(me, 1)] = jnp.full((1,) + table.shape, -1, jnp.int32)
     q_in[pl.ds(me, 1)] = jnp.zeros((1, span, width), BF16)
+    arrived[pl.ds(me, 1)] = jnp.zeros((1,) + arrived.shape[1:], BF16)
     pl.semaphore_wait(barrier, groups + 1)
     each_peer(lambda d: table_copy(d, me).start())
     loads[0].wait()
 
     def norm_step(t, c):
-        normed[pl.ds(t * rows, rows)] = rms(tokens[t].astype(F32), gain[...]).astype(BF16)
+        normed[t] = rms(tokens[t].astype(F32), gain[...]).astype(BF16)
         return c
 
     lax.fori_loop(0, steps, norm_step, 0)
@@ -230,7 +243,7 @@
     to_scalar = pltpu.make_async_copy(loc_v, loc, msem.at[0])
     to_scalar.start()
     loads[1].wait()
-    q = dot_nt(normed[...], wbuf[0]).astype(BF16).astype(F32) * size ** (-0.5)
+    q = dot_nt(normed[...].reshape(steps * rows, normed.shape[-1]), wbuf[0]).astype(BF16).astype(F32) * size ** (-0.5)
     q_req[...] = (
         q.reshape(steps, local, BEAMS, width)
         .transpose(1, 0, 2, 3)
@@ -248,10 +261,10 @@
     q_step[...] = q.astype(BF16).reshape(steps, rows, width)
 
     loads[2].wait()
-    k_new[...] = dot_nt(normed[...], wbuf[1]).astype(BF16).reshape(steps, rows, width)
+    k_new[...] = dot_nt(normed[...].reshape(steps * rows, normed.shape[-1]), wbuf[1]).astype(BF16).reshape(steps, rows, width)
     loads[3].wait()
-    v_new[...] = dot_nt(normed[...], wbuf[2]).astype(BF16).reshape(steps, rows, width)
-    gate = jax.nn.log_sigmoid(dot_nt(normed[...], wf[...]) + bias[...])
+    v_new[...] = dot_nt(normed[...].reshape(steps * rows, normed.shape[-1]), wbuf[2]).astype(BF16).reshape(steps, rows, width)
+    gate = jax.nn.log_sigmoid(dot_nt(normed[...].reshape(steps * rows, normed.shape[-1]), wf[...]) + bias[...])
     spread = jnp.where(iota((heads, width), 1) // size == iota((heads, width), 0), 1.0, 0.0)
     f_new[...] = exact_dot(gate, spread).reshape(steps, rows, width)
     dec[...] = decay[...].astype(F32)
@@ -290,7 +303,13 @@
     loads[4].wait()
     loads[5].wait()
     history(q_step, k_new, v_new, f_new, parents, h_numer, h_top, h_total, heads)
-    pair = 2
+    def turn_page(i, c):
+        turned[i] = turn(values[owned + i])
+        return c
+
+    lax.fori_loop(0, SPILL, turn_page, 0)
+
+    pair = 4
 
     def hosted(i, c):
         found = []
@@ -306,12 +325,12 @@
             source = lax.rem(me - (i * pair + u) + groups, groups)
             page = owned + slot[source]
             found.append(
-                (source, page_partial(q_in[source], masks, keys.at[page], values.at[page], bias_of(page)))
+                (source, page_partial(q_in[source], masks, keys.at[page], turned.at[slot[source]], bias_of(page)))
             )
         for source, (numer, _, _, tops, totals) in found:
             for j in range(blocks):
-                sent[source, :, 128 * j : 128 * (j + 1)] = numer[j].astype(BF16)
-            sent[source, :, width:] = pack_stats(tops, totals).astype(BF16)
+                sent[source, span * j : span * (j + 1)] = numer[j].astype(BF16)
+            sent[source, span * blocks :] = pack_stats(tops, totals).astype(BF16)
         for u in range(pair):
             d = i * pair + u
             source = lax.rem(me - d + groups, groups)
@@ -331,7 +350,7 @@
             page = i * unroll + u
             r = lax.rem(request[page], local)
             found.append(
-                (r, page, page_partial(q_req[r], masks, keys.at[page], values.at[page], bias_of(page)))
+                (r, page, page_partial(q_req[r], masks, keys.at[page], turn(values[page]), bias_of(page)))
             )
         for r, page, (numer, top, total, _, _) in found:
             chain(r, page + 1, numer, top, total)
@@ -340,23 +359,41 @@
     lax.fori_loop(0, owned // unroll, own_pages, 0)
 
     shape = (STAT, 2 * width)
-    row, col = iota(shape, 0), iota(shape, 1)
-    second = jnp.where(col >= width, 1, 0)
-    expand = (row // 8 // 3 == second) & (row % 8 == (col - second * width) // size)
+    _, row_head, row_part = stat_lanes(shape, 0, heads)
+    col = iota(shape, 1)
+    is_total = jnp.where(col >= width, 1, 0)
+    expand = (row_part // 3 == is_total) & (row_part < 5) & (row_head == (col - is_total * width) // size)
     expand = jnp.where(expand, 1.0, 0.0).astype(BF16)
-
-    def absorb(d, c):
-        source = peer_of(d)
-        result_copy(source, source).wait_recv()
-        stats = dot(arrived[source, :, width:], expand)
-        cuts = [slice(128 * j, 128 * (j + 1)) for j in range(blocks)]
-        numer = [arrived[source, :, cut].astype(F32) for cut in cuts]
-        top = [stats[:, cut] for cut in cuts]
-        total = [stats[:, width + cut.start : width + cut.stop] for cut in cuts]
-        chain(loc[source, 0], owned + d, numer, top, total)
-        return c
-
-    lax.fori_loop(1, groups, absorb, 0)
+    owner, _, _ = stat_lanes((span // 4, STAT), 1, heads)
+
+    four = 4
+
+    def absorb(i, c):
+        found = []
+        for u in range(four):
+            d = i * four + u
+            source = peer_of(d)
+
+            @pl.when(d > 0)
+            def _():
+                result_copy(source, source).wait_recv()
+
+            packed = arrived[source, span * blocks :].astype(F32)
+            spread_rows = [jnp.where(owner == g, packed, 0.0) for g in range(4)]
+            found.append(jnp.concatenate(spread_rows, axis=0).astype(BF16))
+        stats = dot(jnp.concatenate(found, axis=0), expand)
+        for u in range(four):
+            d = i * four + u
+            source = peer_of(d)
+            part = stats[span * u : span * (u + 1)]
+            cuts = [slice(128 * j, 128 * (j + 1)) for j in range(blocks)]
+            numer = [arrived[source, span * j : span * (j + 1)].astype(F32) for j in range(blocks)]
+            top = [part[:, cut] for cut in cuts]
+            total = [part[:, width + cut.start : width + cut.stop] for cut in cuts]
+            chain(loc[source, 0], owned + 1 + d, numer, top, total)
+        return c
+
+    lax.fori_loop(0, groups // four, absorb, 0)
 
     for r in range(local):
         cut = slice(r * BEAMS, (r + 1) * BEAMS)
@@ -376,7 +413,6 @@
         query_copy(d, me).wait_send()
         result_copy(peer_of(d), me).wait_send()
 
-    each_peer(finish)
 
     mine = pl.ds(pl.multiple_of(core * half, half), half)
     theirs = pl.ds(pl.multiple_of((1 - core) * half, half), half)
@@ -392,8 +428,8 @@
 
     copy_a = lambda t: pair_copy(0, t, a_tx.at[t], a_rx.at[t], sibling)
     copy_b = lambda t: pair_copy(1, t, b_tx.at[t], b_rx.at[t], across)
-    copy_n = lambda t: pair_copy(2, t, normed_ffn.at[t, mine], normed_ffn.at[t, mine], sibling)
-    copy_n_in = lambda t: pair_copy(2, t, normed_ffn.at[t, theirs], normed_ffn.at[t, theirs], sibling)
+    copy_n = lambda t: pair_copy(2, t, normed.at[t, mine], normed.at[t, mine], sibling)
+    copy_n_in = lambda t: pair_copy(2, t, normed.at[t, theirs], normed.at[t, theirs], sibling)
     copy_c = lambda t: pair_copy(3, t, c_tx.at[t], c_rx.at[t], sibling)
     copy_d = lambda t: pair_copy(4, t, d_tx.at[t], d_rx.at[t], across)
     copy_o = lambda t: pair_copy(5, t, out.at[t, mine], out.at[t, mine], sibling)
@@ -424,6 +460,7 @@
         return c
 
     lax.fori_loop(0, steps + 1, lead, 0)
+    each_peer(finish)
     for load in wloads[1:]:
         load.wait()
 
@@ -436,7 +473,7 @@
         copy_b(t).wait_recv()
         res = tokens[t, mine].astype(F32) + (b_tx[t].astype(F32) + b_rx[t].astype(F32))
         residual[t] = res
-        normed_ffn[t, mine] = rms(res, gain_ffn[...]).astype(BF16)
+        normed[t, mine] = rms(res, gain_ffn[...]).astype(BF16)
         copy_n(t).start()
 
         @pl.when(t > 0)
@@ -444,7 +481,7 @@
             down_cross(t - 1)
 
         copy_n_in(t).wait_recv()
-        x = normed_ffn[t]
+        x = normed[t]
         gate = dot(x, wg[...])
         up = dot(x, wu[...])
         hidden = (gate / (1.0 + jnp.exp(-gate)) * up).astype(BF16)
@@ -466,8 +503,12 @@
 
     lax.fori_loop(0, steps, emit, 0)
 
+    def store(t):
+        return pltpu.make_async_copy(out.at[t], result.at[t], osem.at[t])
+
     def settle(t, c):
         copy_o_in(t).wait_recv()
+        store(t).start()
         copy_a(t).wait_send()
         copy_b(t).wait_send()
         copy_n(t).wait_send()
@@ -477,6 +518,8 @@
         return c
 
     lax.fori_loop(0, steps, settle, 0)
+    for t in range(steps):
+        store(t).wait()
 
 
 VM = pl.BlockSpec(memory_space=pltpu.VMEM)
@@ -504,21 +547,22 @@
     ff = w_gate.shape[1]
     sds = jax.ShapeDtypeStruct
     block = (steps, rows, width)
-    chain = (pages - SPILL + groups, span, width)
+    chain = (pages - SPILL + groups + 1, span, width)
     half = (steps, rows // 2, model)
     return pl.pallas_call(
         functools.partial(group_kernel, groups, local, heads),
         out_shape=sds(tokens.shape, BF16),
         in_specs=[SM, SM, HB, VM, HB, HB, HB, VM, VM, VM, HB, HB, VM, HB, VM, HB, HB, HB],
-        out_specs=VM,
+        out_specs=HB,
         scratch_shapes=[
+            pltpu.VMEM(tokens.shape, BF16),
             pltpu.VMEM(block, BF16),
             pltpu.VMEM(tokens.shape, BF16),
             pltpu.VMEM((3, width, model), BF16),
             pltpu.VMEM(keys_pool.shape, BF16),
             pltpu.VMEM(values_pool.shape, BF16),
             pltpu.VMEM((heads, pages, 128), F32),
-            pltpu.VMEM((steps * rows, model), BF16),
+            pltpu.VMEM(tokens.shape, BF16),
             pltpu.VMEM((local, span, width), BF16),
             pltpu.VMEM(block, BF16),
             pltpu.VMEM(block, BF16),
@@ -529,11 +573,12 @@
             pltpu.VMEM((groups, 128), jnp.int32),
             pltpu.VMEM((groups, span, width), BF16),
             pltpu.VMEM((groups, span, width), BF16),
-            pltpu.VMEM((groups, span, width + STAT), BF16),
-            pltpu.VMEM((groups, span, width + STAT), BF16),
+            pltpu.VMEM((groups, span * width // 128 + span // 4, 128), BF16),
+            pltpu.VMEM((groups, span * width // 128 + span // 4, 128), BF16),
         ]
         + [pltpu.VMEM(chain, F32)] * 3
         + [pltpu.VMEM(block, F32)] * 4
+        + [pltpu.VMEM((SPILL, 128, width), BF16)]
         + [
             pltpu.SMEM((groups, 128), jnp.int32),
             pltpu.SMEM((local,), jnp.int32),
@@ -549,11 +594,10 @@
             pltpu.VMEM((ff, model), BF16),
             pltpu.VMEM(half, F32),
             pltpu.VMEM(half, F32),
-            pltpu.VMEM(tokens.shape, BF16),
             pltpu.VMEM((rows, model), F32),
         ]
         + [pltpu.VMEM(half, BF16)] * 8
-        + [DMA((4,)), DMA((6, steps)), DMA((6, steps))],
+        + [DMA((4,)), DMA((steps,)), DMA((6, steps)), DMA((6, steps))],
         compiler_params=params(collective_id=0, has_side_effects=True),
         name="layer",
     )(

time: 89.9 us -> 85.8 us (0.954)
  Pallas kernels: 87.1 us -> 83 us
    pallas_call x1, Pallas kernels: 87.1 us -> 83 us  [shards(): pl.pallas_call(functools.partial(group_kernel, groups, local, heads), out...]
where the time goes in v4:
time: 85.8 us; the launch traced here: 85.6 us
  Pallas kernels  83 us (97%)
  local copies, waits for them, and re-layouts  2.65 us (3%)
    pallas_call x1, Pallas kernels, shards(): pl.pallas_call(functools.partial(group_kernel, groups, local, heads), out...  83 us
    unnamed x1, local copies, waits for them, and re-layouts  2.65 us

profile of v4, /device:TPU:1, one launch (start us, length us, event | category | flops | bytes accessed | tf_op | source)
XLA Modules:
  0.0 85.6 jit_solution(16684516702527976032)
XLA Ops:
  0.0 83.0 %layer.1 = bf16[4,128,1536]{2,1,0:T(8,128)(2,1)} custom-call(s32[48]{0:T(128)} %request.1, s32[48]{0:T(128)} %fill.1, bf16[4,128,1536]{2,1,0:T(8,128)(2,1)} %tokens_h.1, f32[1536]{0:T(1024)} %gain.1, bf16[384,1536]{1,0:T(8,128)(2,1)} %wq.1, bf16[384,1536]{1,0:T(8,128)(2,1)} %wk.1, bf16[384,1536]{1,0:T(8,128)(2,1)} %wv.1, bf16[6,1536]{1,0:T(8,128)(2,1)} %bitcast.4, ...), custom_call_target="tpu_custom_call" | custom-call | tf_op jit(solution)/shard_map/layer/pallas_call | solution.py:552
  83.0 2.7 %copy.20 = bf16[4,128,1536]{2,1,0:T(8,128)(2,1)} copy(bf16[4,128,1536]{2,1,0:T(8,128)(2,1)} %layer.1) | data formatting | bytes 3145728

commit v5 on v4

--- a/solution.py
+++ b/solution.py
@@ -123,16 +123,18 @@
 
 
 def group_kernel(
-    groups, local, heads, request, fill, tokens_h, gain, wq, wk, wv, wf, bias, parents, keys_h, values_h, decay,
-    wo_h, gain_ffn, wg_h, wu_h, wd_h,
+    groups, local, heads, request, fill, tokens_h, gain_h, wq, wk, wv, wf_h, bias_h, parents_h, keys_h, values_h, decay_h,
+    wo_h, gain_ffn_h, wg_h, wu_h, wd_h,
     result,
-    out, att, tokens, wbuf, keys, values, dec, normed, q_req, q_step, k_new, v_new, f_new,
-    table, table_in, loc_v, send, q_in, sent, arrived, s_numer, s_top, s_total, h_numer, h_top, h_total, final,
+    out, att_all, tokens, wbuf, keys, values, dec, normed, q_req, q_step, k_new, v_new, f_new,
+    table, table_in, loc_v, send, q_in, sent, arrived, s_numer, s_top, s_total, h_numer, h_top, h_total,
     turned,
     loc, last, slot,
     lsem, msem, tsend, trecv, qsend, qrecv, rsend, rrecv,
-    wo, wg, wu, wd, keep, residual, acc,
-    a_tx, a_rx, b_tx, b_rx, c_tx, c_rx, d_tx, d_rx,
+    wo_all, wg, wu, wd, keep, residual, acc,
+    c_tx, c_rx, d_tx, d_rx,
+    wsend, wrecv,
+    gain, wf, bias, parents, decay, gain_ffn, nsem,
     wsem, osem, sems_s, sems_r,
 ):
     steps, rows, width = q_step.shape
@@ -146,10 +148,13 @@
     head = lax.axis_index("head")
     core = lax.rem(head, 2)
     sibling = {"head": head + 1 - 2 * core}
-    across = {"head": core + 2 * (1 - head // 2)}
+    far = core + 2 * (1 - head // 2)
+    across = {"head": far}
+    diagonal = {"head": far + 1 - 2 * core}
+    beyond = {"group": me + 1 - 2 * lax.rem(me, 2), "head": far}
     wloads = [
         pltpu.make_async_copy(a, b, wsem.at[i])
-        for i, (a, b) in enumerate(((wo_h, wo), (wg_h, wg), (wu_h, wu), (wd_h, wd)))
+        for i, (a, b) in enumerate(((wo_h, wo_all.at[head]), (wg_h, wg), (wu_h, wu), (wd_h, wd)))
     ]
     loads = [
         pltpu.make_async_copy(a, b, lsem.at[i])
@@ -164,8 +169,23 @@
             )
         )
     ]
-    for load in loads[:2]:
+    for load in loads[:2] + wloads[:1]:
         load.start()
+    notes = [
+        pltpu.make_async_copy(a, b, nsem.at[i])
+        for i, (a, b) in enumerate(
+            (
+                (gain_h, gain),
+                (wf_h, wf),
+                (bias_h, bias),
+                (parents_h, parents),
+                (decay_h, decay),
+                (gain_ffn_h, gain_ffn),
+            )
+        )
+    ]
+    for note in notes:
+        note.start()
     barrier = pltpu.get_barrier_semaphore()
 
     def peer_of(d):
@@ -184,7 +204,7 @@
         )
     )
 
-    for other in (sibling, across):
+    for other in (sibling, across, diagonal, beyond):
         pl.semaphore_signal(barrier, inc=1, device_id=other, device_id_type=MESH)
 
     def remote(src, dst, ssem, rsem, d):
@@ -221,16 +241,50 @@
     table_in[pl.ds(me, 1)] = jnp.full((1,) + table.shape, -1, jnp.int32)
     q_in[pl.ds(me, 1)] = jnp.zeros((1, span, width), BF16)
     arrived[pl.ds(me, 1)] = jnp.zeros((1,) + arrived.shape[1:], BF16)
-    pl.semaphore_wait(barrier, groups + 1)
+    pl.semaphore_wait(barrier, groups + 3)
     each_peer(lambda d: table_copy(d, me).start())
+    part = wo_all.shape[1] // 2
+    early = part * 2 // 3
+
+    def weight_copy(kind, ref, device):
+        return pltpu.make_async_remote_copy(
+            src_ref=ref,
+            dst_ref=ref,
+            send_sem=wsend.at[kind],
+            recv_sem=wrecv.at[kind],
+            device_id=device,
+            device_id_type=MESH,
+        )
+
+    out_weights = [
+        weight_copy(0, wo_all.at[head, :early], across),
+        weight_copy(1, wo_all.at[head, part : part + early], beyond),
+        weight_copy(2, wo_all.at[head], sibling),
+        weight_copy(3, wo_all.at[far], sibling),
+        weight_copy(4, wo_all.at[head, early:part], across),
+        weight_copy(5, wo_all.at[head, part + early :], beyond),
+    ]
+    in_weights = [
+        weight_copy(0, wo_all.at[far, :early], across),
+        weight_copy(1, wo_all.at[far, part : part + early], beyond),
+        weight_copy(2, wo_all.at[head + 1 - 2 * core], sibling),
+        weight_copy(3, wo_all.at[far + 1 - 2 * core], sibling),
+        weight_copy(4, wo_all.at[far, early:part], across),
+        weight_copy(5, wo_all.at[far, part + early :], beyond),
+    ]
+    wloads[0].wait()
+    for copy in out_weights[:3]:
+        copy.start()
     loads[0].wait()
+    for note in notes:
+        note.wait()
 
     def norm_step(t, c):
         normed[t] = rms(tokens[t].astype(F32), gain[...]).astype(BF16)
         return c
 
     lax.fori_loop(0, steps, norm_step, 0)
-    for load in loads[2:] + wloads:
+    for load in loads[2:] + wloads[1:]:
         load.start()
     each_peer(lambda d: table_copy(d, lax.rem(me + d, groups)).wait_recv())
     batch = 8
@@ -342,6 +396,8 @@
         return c
 
     lax.fori_loop(0, groups // pair, hosted, 0)
+    out_weights[4].start()
+    out_weights[5].start()
     unroll = 4
 
     def own_pages(i, c):
@@ -357,6 +413,10 @@
         return c
 
     lax.fori_loop(0, owned // unroll, own_pages, 0)
+    for i in (0, 1, 4, 5):
+        in_weights[i].wait_recv()
+    out_weights[3].start()
+
 
     shape = (STAT, 2 * width)
     _, row_head, row_part = stat_lanes(shape, 0, heads)
@@ -405,8 +465,8 @@
         h_scale = jnp.exp(h_top[:, cut] - best)
         whole = s_total[entry].reshape(shape) * p_scale + h_total[:, cut] * h_scale
         mixed = s_numer[entry].reshape(shape) * p_scale + h_numer[:, cut] * h_scale
-        final[:, cut] = mixed / whole
-    att[...] = final[...].astype(BF16)
+        h_numer[:, cut] = mixed / whole
+    att_all[head] = h_numer[...].astype(BF16)
 
     def finish(d):
         table_copy(d, me).wait_send()
@@ -426,8 +486,14 @@
             device_id_type=MESH,
         )
 
-    copy_a = lambda t: pair_copy(0, t, a_tx.at[t], a_rx.at[t], sibling)
-    copy_b = lambda t: pair_copy(1, t, b_tx.at[t], b_rx.at[t], across)
+    copy_a = lambda t: pair_copy(1, t, att_all.at[head, t, mine], att_all.at[head, t, mine], across)
+    copy_a_in = lambda t: pair_copy(1, t, att_all.at[far, t, mine], att_all.at[far, t, mine], across)
+    near = head + 1 - 2 * core
+    cross = far + 1 - 2 * core
+    copy_b = lambda t: pair_copy(6, t, att_all.at[head, t, theirs], att_all.at[head, t, theirs], diagonal)
+    copy_b_in = lambda t: pair_copy(6, t, att_all.at[cross, t, mine], att_all.at[cross, t, mine], diagonal)
+    copy_s = lambda t: pair_copy(0, t, att_all.at[head, t, theirs], att_all.at[head, t, theirs], sibling)
+    copy_s_in = lambda t: pair_copy(0, t, att_all.at[near, t, mine], att_all.at[near, t, mine], sibling)
     copy_n = lambda t: pair_copy(2, t, normed.at[t, mine], normed.at[t, mine], sibling)
     copy_n_in = lambda t: pair_copy(2, t, normed.at[t, theirs], normed.at[t, theirs], sibling)
     copy_c = lambda t: pair_copy(3, t, c_tx.at[t], c_rx.at[t], sibling)
@@ -435,31 +501,17 @@
     copy_o = lambda t: pair_copy(5, t, out.at[t, mine], out.at[t, mine], sibling)
     copy_o_in = lambda t: pair_copy(5, t, out.at[t, theirs], out.at[t, theirs], sibling)
 
-    wloads[0].wait()
-
-    def project(t):
-        acc[...] = dot(att[t], wo[...])
-        keep[t] = acc[mine]
-        a_tx[t] = acc[theirs].astype(BF16)
+    def lead(t, c):
         copy_a(t).start()
-
-    def cross(t):
-        copy_a(t).wait_recv()
-        b_tx[t] = (keep[t] + a_rx[t].astype(F32)).astype(BF16)
         copy_b(t).start()
-
-    def lead(t, c):
-        @pl.when(t < steps)
-        def _():
-            project(t)
-
-        @pl.when(t > 0)
-        def _():
-            cross(t - 1)
-
-        return c
-
-    lax.fori_loop(0, steps + 1, lead, 0)
+        copy_s(t).start()
+        return c
+
+    lax.fori_loop(0, steps, lead, 0)
+    in_weights[2].wait_recv()
+    in_weights[3].wait_recv()
+    for copy in out_weights:
+        copy.wait_send()
     each_peer(finish)
     for load in wloads[1:]:
         load.wait()
@@ -470,8 +522,12 @@
         copy_d(t).start()
 
     def feed(t, c):
-        copy_b(t).wait_recv()
-        res = tokens[t, mine].astype(F32) + (b_tx[t].astype(F32) + b_rx[t].astype(F32))
+        copy_a_in(t).wait_recv()
+        copy_b_in(t).wait_recv()
+        copy_s_in(t).wait_recv()
+        res = tokens[t, mine].astype(F32)
+        for h in range(wo_all.shape[0]):
+            res = res + dot(att_all[h, t, mine], wo_all[h])
         residual[t] = res
         normed[t, mine] = rms(res, gain_ffn[...]).astype(BF16)
         copy_n(t).start()
@@ -511,6 +567,7 @@
         store(t).start()
         copy_a(t).wait_send()
         copy_b(t).wait_send()
+        copy_s(t).wait_send()
         copy_n(t).wait_send()
         copy_c(t).wait_send()
         copy_d(t).wait_send()
@@ -526,7 +583,7 @@
 SM = pl.BlockSpec(memory_space=pltpu.SMEM)
 HB = pl.BlockSpec(memory_space=pl.ANY)
 DMA = pltpu.SemaphoreType.DMA
-LIMIT = 60 << 20
+LIMIT = 62 << 20
 
 
 def params(**kw):
@@ -552,11 +609,11 @@
     return pl.pallas_call(
         functools.partial(group_kernel, groups, local, heads),
         out_shape=sds(tokens.shape, BF16),
-        in_specs=[SM, SM, HB, VM, HB, HB, HB, VM, VM, VM, HB, HB, VM, HB, VM, HB, HB, HB],
+        in_specs=[SM, SM] + [HB] * 16,
         out_specs=HB,
         scratch_shapes=[
             pltpu.VMEM(tokens.shape, BF16),
-            pltpu.VMEM(block, BF16),
+            pltpu.VMEM((lax.axis_size("head"),) + block, BF16),
             pltpu.VMEM(tokens.shape, BF16),
             pltpu.VMEM((3, width, model), BF16),
             pltpu.VMEM(keys_pool.shape, BF16),
@@ -577,7 +634,7 @@
             pltpu.VMEM((groups, span * width // 128 + span // 4, 128), BF16),
         ]
         + [pltpu.VMEM(chain, F32)] * 3
-        + [pltpu.VMEM(block, F32)] * 4
+        + [pltpu.VMEM(block, F32)] * 3
         + [pltpu.VMEM((SPILL, 128, width), BF16)]
         + [
             pltpu.SMEM((groups, 128), jnp.int32),
@@ -588,7 +645,7 @@
         ]
         + [DMA((groups,))] * 6
         + [
-            pltpu.VMEM((width, model), BF16),
+            pltpu.VMEM((lax.axis_size("head"), width, model), BF16),
             pltpu.VMEM((model, ff), BF16),
             pltpu.VMEM((model, ff), BF16),
             pltpu.VMEM((ff, model), BF16),
@@ -596,8 +653,18 @@
             pltpu.VMEM(half, F32),
             pltpu.VMEM((rows, model), F32),
         ]
-        + [pltpu.VMEM(half, BF16)] * 8
-        + [DMA((4,)), DMA((steps,)), DMA((6, steps)), DMA((6, steps))],
+        + [pltpu.VMEM(half, BF16)] * 4
+        + [DMA((6,)), DMA((6,))]
+        + [
+            pltpu.VMEM((model,), F32),
+            pltpu.VMEM((heads, model), BF16),
+            pltpu.VMEM((1, heads), F32),
+            pltpu.VMEM(parents.shape, jnp.int32),
+            pltpu.VMEM((heads, pages, 128), BF16),
+            pltpu.VMEM((model,), F32),
+            DMA((6,)),
+        ]
+        + [DMA((4,)), DMA((steps,)), DMA((7, steps)), DMA((7, steps))],
         compiler_params=params(collective_id=0, has_side_effects=True),
         name="layer",
     )(

time: 85.8 us -> 82.4 us (0.960)
  Pallas kernels: 83 us -> 79.6 us
    pallas_call x1, Pallas kernels: 83 us -> 79.6 us  [shards(): pl.pallas_call(functools.partial(group_kernel, groups, local, heads), out...]
where the time goes in v5:
time: 82.4 us; the launch traced here: 82.3 us
  Pallas kernels  79.6 us (97%)
  local copies, waits for them, and re-layouts  2.65 us (3%)
    pallas_call x1, Pallas kernels, shards(): pl.pallas_call(functools.partial(group_kernel, groups, local, heads), out...  79.6 us
    unnamed x1, local copies, waits for them, and re-layouts  2.65 us

profile of v5, /device:TPU:1, one launch (start us, length us, event | category | flops | bytes accessed | tf_op | source)
XLA Modules:
  0.0 82.3 jit_solution(2917863415126184514)
XLA Ops:
  0.0 79.6 %layer.1 = bf16[4,128,1536]{2,1,0:T(8,128)(2,1)} custom-call(s32[48]{0:T(128)} %request.1, s32[48]{0:T(128)} %fill.1, bf16[4,128,1536]{2,1,0:T(8,128)(2,1)} %tokens_h.1, f32[1536]{0:T(1024)} %gain_h.1, bf16[384,1536]{1,0:T(8,128)(2,1)} %wq.1, bf16[384,1536]{1,0:T(8,128)(2,1)} %wk.1, bf16[384,1536]{1,0:T(8,128)(2,1)} %wv.1, bf16[6,1536]{1,0:T(8,128)(2,1)} %bitcast.4, ...), custom_call_target="tpu_custom_call" | custom-call | tf_op jit(solution)/shard_map/layer/pallas_call | solution.py:609
  79.6 2.7 %copy.20 = bf16[4,128,1536]{2,1,0:T(8,128)(2,1)} copy(bf16[4,128,1536]{2,1,0:T(8,128)(2,1)} %layer.1) | data formatting | bytes 3145728

commit v6 on v5

--- a/solution.py
+++ b/solution.py
@@ -273,7 +273,7 @@
         weight_copy(5, wo_all.at[far, part + early :], beyond),
     ]
     wloads[0].wait()
-    for copy in out_weights[:3]:
+    for copy in out_weights[:2]:
         copy.start()
     loads[0].wait()
     for note in notes:
@@ -415,6 +415,7 @@
     lax.fori_loop(0, owned // unroll, own_pages, 0)
     for i in (0, 1, 4, 5):
         in_weights[i].wait_recv()
+    out_weights[2].start()
     out_weights[3].start()
 
 
@@ -521,7 +522,7 @@
         d_tx[t] = (keep[t] + c_rx[t].astype(F32)).astype(BF16)
         copy_d(t).start()
 
-    def feed(t, c):
+    def mix(t):
         copy_a_in(t).wait_recv()
         copy_b_in(t).wait_recv()
         copy_s_in(t).wait_recv()
@@ -532,10 +533,7 @@
         normed[t, mine] = rms(res, gain_ffn[...]).astype(BF16)
         copy_n(t).start()
 
-        @pl.when(t > 0)
-        def _():
-            down_cross(t - 1)
-
+    def feed(t, c):
         copy_n_in(t).wait_recv()
         x = normed[t]
         gate = dot(x, wg[...])
@@ -545,10 +543,16 @@
         keep[t] = acc[mine]
         c_tx[t] = acc[theirs].astype(BF16)
         copy_c(t).start()
-        return c
-
+
+        @pl.when(t + 1 < steps)
+        def _():
+            mix(t + 1)
+
+        down_cross(t)
+        return c
+
+    mix(0)
     lax.fori_loop(0, steps, feed, 0)
-    down_cross(steps - 1)
 
     def emit(t, c):
         copy_d(t).wait_recv()

time: 82.4 us -> 82.4 us (level)
  no operation moved by 1% of the time
where the time goes in v6:
time: 82.4 us; the launch traced here: 82.3 us
  Pallas kernels  79.6 us (97%)
  local copies, waits for them, and re-layouts  2.65 us (3%)
    pallas_call x1, Pallas kernels, shards(): pl.pallas_call(functools.partial(group_kernel, groups, local, heads), out...  79.6 us
    unnamed x1, local copies, waits for them, and re-layouts  2.65 us

profile of v6, /device:TPU:1, one launch (start us, length us, event | category | flops | bytes accessed | tf_op | source)
XLA Modules:
  0.0 82.3 jit_solution(11698678005876091091)
XLA Ops:
  0.0 79.6 %layer.1 = bf16[4,128,1536]{2,1,0:T(8,128)(2,1)} custom-call(s32[48]{0:T(128)} %request.1, s32[48]{0:T(128)} %fill.1, bf16[4,128,1536]{2,1,0:T(8,128)(2,1)} %tokens_h.1, f32[1536]{0:T(1024)} %gain_h.1, bf16[384,1536]{1,0:T(8,128)(2,1)} %wq.1, bf16[384,1536]{1,0:T(8,128)(2,1)} %wk.1, bf16[384,1536]{1,0:T(8,128)(2,1)} %wv.1, bf16[6,1536]{1,0:T(8,128)(2,1)} %bitcast.4, ...), custom_call_target="tpu_custom_call" | custom-call | tf_op jit(solution)/shard_map/layer/pallas_call | solution.py:613
  79.6 2.7 %copy.20 = bf16[4,128,1536]{2,1,0:T(8,128)(2,1)} copy(bf16[4,128,1536]{2,1,0:T(8,128)(2,1)} %layer.1) | data formatting | bytes 3145728
